TPU v7x, 32 devices: a whole 2x2x4 slice. The times are simulated.
32 devices in a mesh: tens: 2 (over y), atom: 16 (over z, x, core).
Axes of the slice: x: 2, y: 2, z: 4, core: 2. Of those that a mesh axis runs over, the one named last changes fastest.
Arguments:
- chibar: float32 [96, 4096], P(None, 'atom'), may hold values from -6 to 6
- t_blocks: float32 [384, 196608], P(None, ('tens', 'atom')), may hold values from -0.3125 to 0.3125
- n_saved: float32 [96, 196608], P('tens', 'atom'), may hold values from -0.078125 to 0.078125
- q_list: int32 [2, 16, 3], P('tens', 'atom'), may hold values from 0 to 13, as said below
- q_count: int32 [2, 16], P('tens', 'atom'), may hold values from 1 to 3, as said below
Outputs:
- gbar: float32 [1024, 320], P('atom')
Inputs may be any that keep to these rules, and one draw needn't show every extreme that they name: `q_list`: the 3 entries of one pair owner's list name blocks of 3 distinct atom indices. `q_count`: equal to 3 on at least one pair owner.
All inputs are finite; a program needn't handle non-finite values.
Results may differ from a plain program's by a relative error of at most 0.0003.
Values sent between devices are 32-bit elements; how exact they have to be, the bound alone decides.
No kernel may reach another device: no remote copies, remote signals or barrier semaphores. Data moves between devices by JAX's collectives and lax.ppermute only.
A program may use at most 64 MiB of HBM per device.

v0:
```python
import jax
import jax.numpy as jnp
from jax import lax
from jax.experimental import pallas as pl
from jax.experimental.pallas import tpu as pltpu
from jax.sharding import PartitionSpec as P


LANES = 128
SUBL = 8
REACH = 3
EARLY_PART = 8
VM = pl.BlockSpec(memory_space=pltpu.VMEM)
HB = pl.BlockSpec(memory_space=pltpu.HBM)
f32 = jnp.float32
bf16 = jnp.bfloat16


def limit(mib):
    return pltpu.CompilerParams(vmem_limit_bytes=mib * 2**20)


def vmem(shape, dtype):
    return pltpu.VMEM(shape, dtype)


def split(x):
    hi = x.astype(bf16)
    return hi, (x - hi.astype(f32)).astype(bf16)


def shift(x, by):
    atoms = lax.axis_size("atom")
    return lax.ppermute(x, "atom", [(i, (i + by) % atoms) for i in range(atoms)])


def send(x, to):
    atoms = lax.axis_size("atom")
    pairs = []
    for t in range(2):
        for s in range(atoms):
            u, v = to(t, s)
            pairs.append((t * atoms + s, u * atoms + v % atoms))
    return lax.ppermute(x, ("tens", "atom"), pairs)


def neighbours(x):
    atoms = lax.axis_size("atom")
    pair = [(i, i ^ 1) for i in range(atoms)]

    def move(y, pairs):
        return lax.ppermute(y, "atom", pairs)

    far = move(x, [(i, (i + (3 if i % 2 else -3)) % atoms) for i in range(atoms)])
    below = move(x, [(i, (i + 2) % atoms) for i in range(atoms)])
    above = move(x, [(i, (i - 2) % atoms) for i in range(atoms)])
    partner = move(x, pair)
    return [far, below, move(below, pair), x, partner, above, move(above, pair)]


def prep_t(t_blocks, first, slope, cols, *early):
    rows = t_blocks.shape[0]
    step = 64
    sub = 512 if cols % 512 == 0 else LANES

    def body(src, *refs):
        hi, lo, buf, sems = refs[len(early):]
        start = pl.multiple_of(first + slope * lax.axis_index("tens"), LANES)
        copies = []
        for i in range(rows // step):
            here = pl.ds(i * step, step)
            copies.append(pltpu.make_async_copy(src.at[here, pl.ds(start, cols)], buf.at[here], sems.at[i]))
            copies[-1].start()
        for i in range(rows // step):
            copies[i].wait()

            def tile(c, carry, i=i):
                at = pl.ds(pl.multiple_of(c * sub, sub), sub)
                here = pl.ds(i * step, step)
                h, l = split(buf[here, at])
                hi[here, at] = h
                lo[here, at] = l
                return carry

            lax.fori_loop(0, cols // sub, tile, 0)

    return pl.pallas_call(
        body, in_specs=[HB] + [VM] * len(early), out_specs=[VM, VM],
        out_shape=[vmem((rows, cols), bf16), vmem((rows, cols), bf16)],
        scratch_shapes=[pltpu.VMEM((rows, cols), f32), pltpu.SemaphoreType.DMA((rows // step,))],
        name="prep_t", compiler_params=limit(12),
    )(t_blocks, *early)


def head(x, part):
    tiles = x.shape[1] // LANES
    rows = 2 * SUBL

    def body(src, out, buf, sem):
        copy = pltpu.make_async_copy(src.at[pl.ds(0, rows)], buf, sem)
        copy.start()
        copy.wait()
        for c in range(tiles):
            at = pl.ds(c * LANES, LANES)
            out[pl.ds(c * SUBL, SUBL), :] = buf[:SUBL, at]
            out[pl.ds(tiles * SUBL + c * part, part), :] = buf[SUBL:SUBL + part, at]

    return pl.pallas_call(
        body, in_specs=[HB], out_specs=VM, out_shape=vmem((tiles * (SUBL + part), LANES), x.dtype),
        scratch_shapes=[pltpu.VMEM((rows, x.shape[1]), f32), pltpu.SemaphoreType.DMA],
        name="head", compiler_params=limit(4),
    )(x)


def place_row(tiles, first, per, orb, tmp, hi, lo, at):
    half = LANES // 2
    pairs = orb // 2
    low = lax.broadcasted_iota(jnp.int32, (pairs, LANES), 1) < half
    v = [tiles[pl.ds(first + k * per, pairs, stride=3 * per), :] for k in range(3)]
    w1, w2 = (pltpu.roll(x, half, 1) for x in v[1:])
    tmp[0, pl.ds(0, pairs, stride=2), :] = v[0]
    tmp[1, pl.ds(0, pairs, stride=2), :] = v[1]
    tmp[0, pl.ds(1, pairs, stride=2), :] = jnp.where(low, w1, w2)
    tmp[1, pl.ds(1, pairs, stride=2), :] = w2
    for k in range(2):
        h, l = split(tmp[k])
        hi[at, k * LANES:(k + 1) * LANES] = h
        lo[at, k * LANES:(k + 1) * LANES] = l


def prep_n(saved, orb):
    rows, cols = saved.shape
    groups = rows // SUBL

    def body(src, hi, lo, buf, tiles, tmp, sems):
        def copy(i):
            here = pl.ds(pl.multiple_of(i * SUBL, SUBL), SUBL)
            return pltpu.make_async_copy(src.at[here], buf.at[here], sems.at[i])

        for i in range(groups):
            copy(i).start()

        def group(i, carry):
            copy(i).wait()
            here = pl.ds(pl.multiple_of(i * SUBL, SUBL), SUBL)
            for c in range(cols // LANES):
                tiles[c * SUBL:(c + 1) * SUBL, :] = buf[here, c * LANES:(c + 1) * LANES]
            for r in range(SUBL):
                at = pl.ds(pl.multiple_of(i * SUBL * orb + r * orb, orb), orb)
                place_row(tiles, r, SUBL, orb, tmp.at[r], hi, lo, at)
            return carry

        lax.fori_loop(0, groups, group, 0)

    return pl.pallas_call(
        body, in_specs=[HB], out_specs=[VM, VM],
        out_shape=[vmem((rows * orb, 2 * LANES), bf16)] * 2,
        scratch_shapes=[pltpu.VMEM((rows, cols), f32), pltpu.VMEM((cols // LANES * SUBL, LANES), f32),
                        pltpu.VMEM((SUBL, 2, orb, LANES), f32), pltpu.SemaphoreType.DMA((groups,))],
        name="prep_n", compiler_params=limit(10),
    )(saved)


def prep_far(packed, part, orb):
    rows = SUBL + part
    tiles = packed.shape[0] // rows

    def body(src, hi, lo, tmp):
        for p in range(rows):
            first, per = (p, SUBL) if p < SUBL else (tiles * SUBL + p - SUBL, part)
            place_row(src, first, per, orb, tmp.at[p], hi, lo, pl.ds(p * orb, orb))

    return pl.pallas_call(
        body, in_specs=[VM], out_specs=[VM, VM], out_shape=[vmem((rows * orb, 2 * LANES), bf16)] * 2,
        scratch_shapes=[pltpu.VMEM((rows, 2, orb, LANES), f32)], name="prep_far", compiler_params=limit(6),
    )(packed)


def select(pieces, q_list, q_count, p_rows, early):
    p_all, width = pieces[0].shape
    ql = q_list.shape[-1]
    blk = LANES
    qb = width // blk

    def body(*refs):
        parts, (list_ref, count_ref, out, scr) = refs[:len(pieces)], refs[len(pieces):]
        t = lax.axis_index("tens")
        s = lax.axis_index("atom")
        for q in range(ql):
            used = jnp.where(count_ref[...] > q, list_ref[0][:, q:q + 1], -1)
            turned = (((used >> 1) & 1) == 0) & (s % 2 == 1)
            used = jnp.where(turned, 2 * (((used >> 1) + 2) & 7) + (used & 1), used)
            want = jnp.broadcast_to(used, (1, blk))
            pick = jnp.zeros((p_all, blk), f32)
            for i in range(len(parts) * qb):
                pick = jnp.where(want == i, parts[i // qb][:, (i % qb) * blk:(i % qb + 1) * blk], pick)
            scr[:, q * blk:(q + 1) * blk] = pick
        other = (1 - t) * p_rows
        order = ((other + early, p_rows - early), (t * p_rows, p_rows), (other, early))
        at = 0
        for start, size in order:
            h, l = split(scr[pl.ds(pl.multiple_of(start, 16), size), :])
            out[at:at + size, :] = h
            out[p_all + at:p_all + at + size, :] = l
            at += size

    return pl.pallas_call(
        body, in_specs=[VM] * (len(pieces) + 2), out_specs=VM,
        out_shape=vmem((2 * p_all, ql * blk), bf16),
        scratch_shapes=[pltpu.VMEM((p_all, ql * blk), f32)], name="select", compiler_params=limit(8),
    )(*pieces, q_list, q_count)


def multiply(chosen, t_parts, p_rows, part):
    p_all = chosen.shape[0] // 2
    cols = t_parts[0][0].shape[1]
    ct = cols * len(t_parts) // LANES
    sub = 512 if cols % 512 == 0 else 256
    far_full = p_rows // SUBL - 2
    own_full = p_all // SUBL - far_full - 1

    def body(c, *refs):
        out_c, out_o = refs[-2:]
        for j in range(cols * len(t_parts) // sub):
            which = j * sub // cols
            hi, lo = refs[2 * which:2 * which + 2]
            at = pl.ds(j * sub - which * cols, sub)
            big = jnp.dot(c[...], hi[:, at], preferred_element_type=f32)
            val = big[:p_all] + big[p_all:] + jnp.dot(c[:p_all, :], lo[:, at], preferred_element_type=f32)
            for k in range(sub // LANES):
                jt = j * (sub // LANES) + k
                for i in range(p_all // SUBL):
                    v = val[i * SUBL:(i + 1) * SUBL, k * LANES:(k + 1) * LANES]
                    if i < far_full:
                        out_c[pl.ds((i * ct + jt) * SUBL, SUBL), :] = v
                    elif i < far_full + own_full:
                        out_o[pl.ds(((i - far_full) * ct + jt) * SUBL, SUBL), :] = v
                    else:
                        out_o[pl.ds(own_full * ct * SUBL + jt * part, part), :] = v[:part]
                        rest = SUBL - part
                        if rest:
                            out_c[pl.ds(far_full * ct * SUBL + jt * rest, rest), :] = v[part:]

    return pl.pallas_call(
        body, in_specs=[VM] * (1 + 2 * len(t_parts)), out_specs=[VM, VM],
        out_shape=[vmem(((far_full * SUBL + SUBL - part) * ct, LANES), f32),
                   vmem(((own_full * SUBL + part) * ct, LANES), f32)],
        name="multiply", compiler_params=limit(8),
    )(chosen, *[x for part in t_parts for x in part])


def contract_into(x, rows, ct, n_parts, n_rows, left):
    lane = lax.broadcasted_iota(jnp.int32, (ct, LANES), 1)
    low = lane < LANES // 2
    tail = rows % SUBL

    def row(q):
        per = SUBL if q < rows - tail else tail
        return x[pl.ds((q // SUBL) * ct * SUBL + q % SUBL, ct, stride=per), :]

    for p in range(0, rows, 2):
        a, b = row(p), row(p + 1)
        even = jnp.where(low, a, pltpu.roll(b, LANES // 2, 1))
        odd = jnp.where(low, pltpu.roll(a, LANES // 2, 1), b)
        at = pl.ds((p // 2) * LANES, LANES)
        for i, v in enumerate((even, odd)):
            h, l = split(v)
            left[pl.ds(i * ct, ct), at] = h
            left[pl.ds((2 + i) * ct, ct), at] = l
    half = LANES // 2
    total = None
    at = 0
    for (w_hi, w_lo), (start, count) in zip(n_parts, n_rows):
        k = pl.ds(at * half, count * half)
        w = pl.ds(start * half, count * half)
        both = jnp.dot(left[:, k], w_hi[w, :], preferred_element_type=f32)
        v = both[:2 * ct] + both[2 * ct:]
        v += jnp.dot(left[:2 * ct, k], w_lo[w, :], preferred_element_type=f32)
        total = v if total is None else total + v
        at += count
    return total


def contract(stretches, rows, saved, n_rows, band, sizes, after=()):
    wide = -(-band // LANES)
    cts = [x.shape[0] // rows for x in stretches]
    flat = [w for pair in saved for w in pair]

    def body(*refs):
        refs = list(refs)
        xs = [refs.pop(0) for _ in stretches]
        ws = [refs.pop(0) for _ in flat]
        del refs[:len(after)]
        outs = [refs.pop(0) for _ in sizes]
        acc = refs.pop(0)
        pairs = list(zip(ws[0::2], ws[1::2]))
        base = 0
        for i, (x, ct) in enumerate(zip(xs, cts)):
            val = contract_into(x, rows, ct, pairs, n_rows, refs[i])
            for par in range(2):
                for c in range(wide):
                    acc[c, pl.ds(base + par, ct, stride=2), :] = val[par * ct:(par + 1) * ct, c * LANES:(c + 1) * LANES]
            base += 2 * ct
        at = 0
        for out, size in zip(outs, sizes):
            half = size // 2
            low = lax.broadcasted_iota(jnp.int32, (half, LANES), 1) < LANES // 2
            out[:size, :] = acc[0, at:at + size, :]
            out[size:, :] = jnp.where(low, acc[1, at:at + half, :], pltpu.roll(acc[1, at + half:at + size, :], LANES // 2, 1))
            at += size

    scratch = [pltpu.VMEM((wide, 2 * sum(cts), LANES), f32)]
    for x, ct in zip(stretches, cts):
        scratch.append(pltpu.VMEM((4 * ct, rows * LANES // 2), bf16))
    return pl.pallas_call(
        body, in_specs=[VM] * (len(stretches) + len(flat) + len(after)), out_specs=[VM] * len(sizes),
        out_shape=[vmem((size * band // LANES, LANES), f32) for size in sizes], scratch_shapes=scratch,
        name="contract", compiler_params=limit(12),
    )(*stretches, *flat, *after)


def unpack(x, size, band):
    low = x[size:]
    tail = jnp.concatenate([low, pltpu.roll(low, LANES // 2, 1)], axis=0)
    return jnp.concatenate([x[:size], tail], axis=1)[:, :band]


def finish(own, rec, orb, band):
    def body(ho, oa, ob, oc, hr, ra, rb, rc, out):
        first = lax.axis_index("tens") == 0
        lower = jnp.where(first, ob[...], oa[...]) + jnp.where(first, ra[...], rb[...])
        upper = jnp.where(first, oa[...], ob[...]) + jnp.where(first, rb[...], ra[...])
        x = ho[...] + rc[...]
        y = oc[...] + hr[...]
        rest = x.shape[0] * LANES // band
        x, y = unpack(jnp.where(first, x, y), rest, band), unpack(jnp.where(first, y, x), rest, band)
        lower, upper = unpack(lower, orb, band), unpack(upper, orb, band)
        zero = jnp.zeros((orb, orb), f32)
        out[...] = (jnp.concatenate([lower, zero, zero], axis=1)
                    + jnp.concatenate([zero, jnp.concatenate([x, y], axis=0), zero], axis=1)
                    + jnp.concatenate([zero, zero, upper], axis=1))

    return pl.pallas_call(
        body, in_specs=[VM] * 8, out_specs=VM,
        out_shape=jax.ShapeDtypeStruct((orb, band + 2 * orb), f32), name="finish", compiler_params=limit(8),
    )(*own, *rec)


def paired(chibar, t_blocks, n_saved, q_list, q_count):
    p_rows, n_cols = n_saved.shape
    orb = LANES // 2
    band = n_cols // orb
    nu_t = t_blocks.shape[1] // orb
    part = EARLY_PART
    early = SUBL + part
    cross = p_rows - early
    swap = [(0, 1), (1, 0)]

    n_saved = pltpu.with_memory_space_constraint(n_saved, pltpu.HBM)
    t_blocks = pltpu.with_memory_space_constraint(t_blocks, pltpu.HBM)
    n_far = lax.ppermute(head(n_saved, part), "tens", swap)
    pieces = neighbours(chibar)
    rest = nu_t - orb
    half = orb * orb // 2
    t_main = [prep_t(t_blocks, 0, rest * orb, half, q_count)]
    t_main.append(prep_t(t_blocks, half, rest * orb, half))
    chosen = select(pieces, q_list, q_count, p_rows, 2 * SUBL)
    far_main, own_main = multiply(chosen, t_main, p_rows, part)
    far_main = lax.ppermute(far_main, "tens", swap)
    t_rest = prep_t(t_blocks, orb * orb, -orb * orb, rest * orb)
    far_rest, own_rest = multiply(chosen, [t_rest], p_rows, part)
    far_rest = lax.ppermute(far_rest, "tens", swap)

    near = prep_n(n_saved, orb)
    beyond = prep_far(n_far, part, orb)
    far_rows = [(2 * SUBL, p_rows - 2 * SUBL), (early, SUBL - part)][:2 if part < SUBL else 1]
    o_main, o_rest = contract([own_main, own_rest], p_rows + early, [near, beyond], [(0, p_rows), (0, early)],
                              band, [orb, rest])
    oa = send(o_main, lambda t, s: (t, s - 1 + 2 * t))
    ob = send(o_main, lambda t, s: (1 - t, s - 1 + 2 * t))
    oc = send(o_rest, lambda t, s: (1 - t, s))
    r_main, = contract([far_main], cross, [near, near], far_rows, band, [orb], after=(o_rest,))
    ra = send(r_main, lambda t, s: (t, s + 1 - 2 * t))
    rb = send(r_main, lambda t, s: (1 - t, s + 1 - 2 * t))
    r_rest, = contract([far_rest], cross, [near, near], far_rows, band, [rest])
    rc = send(r_rest, lambda t, s: (1 - t, s))
    return finish((o_rest, oa, ob, oc), (r_rest, ra, rb, rc), orb, band)


def general(chibar, t_blocks, n_saved, q_list, q_count):
    tens = lax.axis_size("tens")
    t = lax.axis_index("tens")
    p_rows, n_cols = n_saved.shape
    blk = t_blocks.shape[0] // q_list.shape[-1]
    ql = q_list.shape[-1]
    qb = chibar.shape[1] // blk
    reach = REACH
    orb = int(round((n_cols // 3) ** 0.5))
    band = 3 * orb
    nu_t = t_blocks.shape[1] // orb
    high = lax.Precision.HIGH
    slot_ids = q_list.reshape(ql)
    in_use = q_count.reshape(())
    keeper = jnp.arange(ql) < in_use

    def chosen_of(r):
        rows = lax.dynamic_slice_in_dim(chibar, ((t + r) % tens) * p_rows, p_rows, 0)
        pieces = [rows if o == 0 else shift(rows, -o) for o in range(-reach, reach + 1)]
        blocks = [pc[:, b * blk:(b + 1) * blk] for pc in pieces for b in range(qb)]
        out = []
        for q in range(ql):
            pick = blocks[0]
            for i in range(1, len(blocks)):
                pick = jnp.where(slot_ids[q] == i, blocks[i], pick)
            out.append(jnp.where(keeper[q], pick, 0.0))
        return jnp.concatenate(out, axis=1)

    saved = n_saved.reshape(p_rows, orb, band)
    parts = []
    mb = []
    for r in list(range(1, tens)) + [0]:
        m = jnp.dot(chosen_of(r), t_blocks, precision=high, preferred_element_type=jnp.float32)
        if r:
            m = lax.ppermute(m, "tens", [(i, (i + r) % tens) for i in range(tens)])
        mb.append(m)
    mb = [mb[-1]] + mb[:-1]
    for r in range(tens):
        parts.append(jnp.einsum("pnm,pml->nl", mb[r].reshape(p_rows, nu_t, orb), saved, precision=high,
                                preferred_element_type=jnp.float32))
    stacked = jnp.stack(parts)
    order = (t - jnp.arange(tens)) % tens
    if tens == 2:
        partial = jnp.where(t == 0, stacked, stacked[::-1]).reshape(band, band)
    else:
        partial = jnp.take(stacked, order, axis=0).reshape(band, band)
    blocks = partial.reshape(3, orb, band)
    lower = shift(blocks[2], 1)
    upper = shift(blocks[0], -1)
    pad = lambda x, o: jnp.pad(x, ((0, 0), (o * orb, (2 - o) * orb)))
    res = pad(lower, 0) + pad(blocks[1], 1) + pad(upper, 2)
    if tens == 2:
        return res + lax.ppermute(res, "tens", [(0, 1), (1, 0)])
    return lax.psum(res, "tens")


def solution(mesh):
    placed = (
        P(None, "atom"),
        P(None, ("tens", "atom")),
        P("tens", "atom"),
        P("tens", "atom", None),
        P("tens", "atom"),
    )

    def program(body):
        return jax.shard_map(body, mesh=mesh, in_specs=placed, out_specs=P("atom", None), check_vma=False)

    if mesh.shape["tens"] != 2 or mesh.shape["atom"] % 2:
        return program(general)

    return program(paired)
```

profile of v0, /device:TPU:0, one launch (start us, length us, event | category | flops | bytes accessed | tf_op | source)
XLA Modules:
  0.0 59.7 jit_solution(1589085173390637202)
XLA Ops:
  0.0 0.0 copy-start
  0.0 1.2 %head.1 = f32[1536,128]{1,0:T(8,128)S(1)} custom-call(f32[48,12288]{1,0:T(8,128)} %src.9), custom_call_target="tpu_custom_call" | custom-call | tf_op jit(solution)/shard_map/head/pallas_call | solution.py:108
  1.2 3.1 %collective-permute-start.6 = (f32[1536,128]{1,0:T(8,128)S(1)}, f32[1536,128]{1,0:T(8,128)S(1)}, u32[]{:S(2)}, u32[]{:S(2)}) collective-permute-start(f32[1536,128]{1,0:T(8,128)S(1)} %head.1), channel_id=1, source_target_pairs={{0,16},{16,0},{1,17},{17,1},{2,18},{18,2},{3,19},{19,3},{4,20},{20... | collective-permute-start | bytes 2359304 | tf_op jit(solution)/shard_map/ppermute | solution.py:361
  4.3 0.0 copy-done
  4.3 1.5 %collective-permute-start.1 = (f32[96,256]{1,0:T(8,128)S(1)}, f32[96,256]{1,0:T(8,128)S(1)}, u32[]{:S(2)}, u32[]{:S(2)}) collective-permute-start(f32[96,256]{1,0:T(8,128)S(1)} %copy-done), channel_id=1, source_target_pairs={{0,2},{1,3},{2,4},{3,5},{4,6},{5,7},{6,8},{7,9},{8,10},{9,11},{10,... | collective-permute-start | bytes 294920 | tf_op jit(solution)/shard_map/ppermute | solution.py:52
  5.8 3.2 %collective-permute-start.4 = (f32[96,256]{1,0:T(8,128)S(1)}, f32[96,256]{1,0:T(8,128)S(1)}, u32[]{:S(2)}, u32[]{:S(2)}) collective-permute-start(f32[96,256]{1,0:T(8,128)S(1)} %copy-done), channel_id=1, source_target_pairs={{0,14},{1,15},{2,0},{3,1},{4,2},{5,3},{6,4},{7,5},{8,6},{9,7},{10,... | collective-permute-start | bytes 294920 | tf_op jit(solution)/shard_map/ppermute | solution.py:52
  9.0 0.4 collective-permute-start
  9.4 0.0 collective-permute-start.3
  9.4 2.3 %collective-permute-done.1.refs_1_ = f32[96,256]{1,0:T(8,128)S(1)} collective-permute-done((f32[96,256]{1,0:T(8,128)S(1)}, f32[96,256]{1,0:T(8,128)S(1)}, u32[]{:S(2)}, u32[]{:S(2)}) %collective-permute-start.1) | collective-permute-done | bytes 98336 | tf_op jit(solution)/shard_map/ppermute | solution.py:52
  11.7 0.0 collective-permute-start.2
  11.7 0.7 %collective-permute-done.4.refs_5_ = f32[96,256]{1,0:T(8,128)S(1)} collective-permute-done((f32[96,256]{1,0:T(8,128)S(1)}, f32[96,256]{1,0:T(8,128)S(1)}, u32[]{:S(2)}, u32[]{:S(2)}) %collective-permute-start.4) | collective-permute-done | bytes 98336 | tf_op jit(solution)/shard_map/ppermute | solution.py:52
  12.4 0.0 collective-permute-start.5
  13.1 2.0 %prep_t.4 = (bf16[384,2048]{1,0:T(8,128)(2,1)S(1)}, bf16[384,2048]{1,0:T(8,128)(2,1)S(1)}) custom-call(f32[384,6144]{1,0:T(8,128)} %src.7), custom_call_target="tpu_custom_call" | custom-call | tf_op jit(solution)/shard_map/prep_t/pallas_call | solution.py:87
  15.0 0.0 copy-start.1
  15.0 2.0 %prep_t.3 = (bf16[384,2048]{1,0:T(8,128)(2,1)S(1)}, bf16[384,2048]{1,0:T(8,128)(2,1)S(1)}) custom-call(f32[384,6144]{1,0:T(8,128)} %src.7, s32[1,1]{1,0:T(1,128)S(6)} %copy.6.refs_8_.refs_0_), custom_call_target="tpu_custom_call" | custom-call | tf_op jit(solution)/shard_map/prep_t/pallas_call | solution.py:87
  17.0 0.0 collective-permute-done.refs_0_
  17.0 0.0 collective-permute-done.3.refs_4_
  17.0 0.0 collective-permute-done.2.refs_2_
  17.0 0.0 collective-permute-done.5.refs_6_
  17.1 0.0 copy-done.1
  17.1 0.2 select.1.c
  17.3 1.5 %multiply.2 = (f32[1024,128]{1,0:T(8,128)S(1)}, f32[2048,128]{1,0:T(8,128)S(1)}) custom-call(bf16[192,384]{1,0:T(8,128)(2,1)S(1)} %select.1.c, bf16[384,2048]{1,0:T(8,128)(2,1)S(1)} %get-tuple-element.21.refs_0_, bf16[384,2048]{1,0:T(8,128)(2,1)S(1)} %get-tuple-element.22.refs_1_, bf16[384,2048]{1,0:T(8,128)(2,1)S(1)} %get-tuple-element.23.refs_2_, ...), custom_call_target="tpu_custom_call" | custom-call | tf_op jit(solution)/shard_map/multiply/pallas_call | solution.py:244
  18.8 0.6 collective-permute-start.11
  19.4 2.0 %prep_t.5 = (bf16[384,2048]{1,0:T(8,128)(2,1)S(1)}, bf16[384,2048]{1,0:T(8,128)(2,1)S(1)}) custom-call(f32[384,6144]{1,0:T(8,128)} %src.7), custom_call_target="tpu_custom_call" | custom-call | tf_op jit(solution)/shard_map/prep_t/pallas_call | solution.py:87
  21.3 0.8 %multiply.3 = (f32[512,128]{1,0:T(8,128)S(1)}, f32[1024,128]{1,0:T(8,128)S(1)}) custom-call(bf16[192,384]{1,0:T(8,128)(2,1)S(1)} %select.1.c, bf16[384,2048]{1,0:T(8,128)(2,1)S(1)} %get-tuple-element.26.refs_0_, bf16[384,2048]{1,0:T(8,128)(2,1)S(1)} %get-tuple-element.27.refs_1_), custom_call_target="tpu_custom_call" | custom-call | tf_op jit(solution)/shard_map/multiply/pallas_call | solution.py:244
  22.2 1.6 %collective-permute-start.10 = (f32[512,128]{1,0:T(8,128)S(1)}, f32[512,128]{1,0:T(8,128)S(1)}, u32[]{:S(2)}, u32[]{:S(2)}) collective-permute-start(f32[512,128]{1,0:T(8,128)S(1)} %get-tuple-element.35), channel_id=1, source_target_pairs={{0,16},{16,0},{1,17},{17,1},{2,18},{18,2},{3,19},{19,3},{4,20},{20... | collective-permute-start | bytes 786440 | tf_op jit(solution)/shard_map/ppermute | solution.py:372
  23.7 2.4 %prep_n.1 = (bf16[3072,256]{1,0:T(8,128)(2,1)S(1)}, bf16[3072,256]{1,0:T(8,128)(2,1)S(1)}) custom-call(f32[48,12288]{1,0:T(8,128)} %src.9), custom_call_target="tpu_custom_call" | custom-call | tf_op jit(solution)/shard_map/prep_n/pallas_call | solution.py:155
  26.2 12.7 %collective-permute-done.10.refs_0_ = f32[512,128]{1,0:T(8,128)S(1)} collective-permute-done((f32[512,128]{1,0:T(8,128)S(1)}, f32[512,128]{1,0:T(8,128)S(1)}, u32[]{:S(2)}, u32[]{:S(2)}) %collective-permute-start.10) | collective-permute-done | bytes 262176 | tf_op jit(solution)/shard_map/ppermute | solution.py:372
  38.8 0.6 contract.4.hr
  39.4 1.6 %collective-permute-start.14 = (f32[48,128]{1,0:T(8,128)S(1)}, f32[48,128]{1,0:T(8,128)S(1)}, u32[]{:S(2)}, u32[]{:S(2)}) collective-permute-start(f32[48,128]{1,0:T(8,128)S(1)} %contract.4.hr), channel_id=1, source_target_pairs={{0,16},{1,17},{2,18},{3,19},{4,20},{5,21},{6,22},{7,23},{8,24},{9,... | collective-permute-start | bytes 73736 | tf_op jit(solution)/shard_map/ppermute | solution.py:44
  41.0 0.0 collective-permute-done.6.src
  41.0 0.4 prep_far.1
  41.4 1.7 %contract.3 = (f32[96,128]{1,0:T(8,128)S(1)}, f32[48,128]{1,0:T(8,128)S(1)}) custom-call(f32[2048,128]{1,0:T(8,128)S(1)} %get-tuple-element.25.refs_0_, f32[1024,128]{1,0:T(8,128)S(1)} %get-tuple-element.28.refs_1_, bf16[3072,256]{1,0:T(8,128)(2,1)S(1)} %get-tuple-element.29.refs_2_.refs_1_.refs_3_, ...), custom_call_target="tpu_custom_call" | custom-call | tf_op jit(solution)/shard_map/contract/pallas_call | solution.py:315
  43.1 0.0 collective-permute-done.11.refs_0_
  43.1 0.6 %contract.5 = f32[96,128]{1,0:T(8,128)S(1)} custom-call(f32[1024,128]{1,0:T(8,128)S(1)} %collective-permute-done.11.refs_0_, bf16[3072,256]{1,0:T(8,128)(2,1)S(1)} %get-tuple-element.29.refs_2_.refs_1_.refs_3_, bf16[3072,256]{1,0:T(8,128)(2,1)S(1)} %get-tuple-element.30.refs_3_.refs_2_.refs_4_, ...), custom_call_target="tpu_custom_call" | custom-call | tf_op jit(solution)/shard_map/contract/pallas_call | solution.py:315
  43.7 0.0 collective-permute-start.12
  43.7 0.5 collective-permute-start.13
  44.2 7.5 %collective-permute-start.7 = (f32[96,128]{1,0:T(8,128)S(1)}, f32[96,128]{1,0:T(8,128)S(1)}, u32[]{:S(2)}, u32[]{:S(2)}) collective-permute-start(f32[96,128]{1,0:T(8,128)S(1)} %get-tuple-element.34), channel_id=1, source_target_pairs={{0,15},{1,0},{2,1},{3,2},{4,3},{5,4},{6,5},{7,6},{8,7},{9,8},{10,9... | collective-permute-start | bytes 147464 | tf_op jit(solution)/shard_map/ppermute | solution.py:44
  51.8 1.7 %collective-permute-start.8 = (f32[96,128]{1,0:T(8,128)S(1)}, f32[96,128]{1,0:T(8,128)S(1)}, u32[]{:S(2)}, u32[]{:S(2)}) collective-permute-start(f32[96,128]{1,0:T(8,128)S(1)} %get-tuple-element.34), channel_id=1, source_target_pairs={{0,31},{1,16},{2,17},{3,18},{4,19},{5,20},{6,21},{7,22},{8,23},{9,... | collective-permute-start | bytes 147464 | tf_op jit(solution)/shard_map/ppermute | solution.py:44
  53.5 0.0 collective-permute-done.14.rc
  53.5 0.0 collective-permute-start.9
  53.5 3.8 %collective-permute-done.9.oc = f32[48,128]{1,0:T(8,128)S(1)} collective-permute-done((f32[48,128]{1,0:T(8,128)S(1)}, f32[48,128]{1,0:T(8,128)S(1)}, u32[]{:S(2)}, u32[]{:S(2)}) %collective-permute-start.9) | collective-permute-done | bytes 24608 | tf_op jit(solution)/shard_map/ppermute | solution.py:44
  57.3 0.0 collective-permute-done.12.ra
  57.3 0.0 collective-permute-done.13.rb
  57.3 0.0 collective-permute-done.7.oa
  57.3 1.5 %collective-permute-done.8.ob = f32[96,128]{1,0:T(8,128)S(1)} collective-permute-done((f32[96,128]{1,0:T(8,128)S(1)}, f32[96,128]{1,0:T(8,128)S(1)}, u32[]{:S(2)}, u32[]{:S(2)}) %collective-permute-start.8) | collective-permute-done | bytes 49184 | tf_op jit(solution)/shard_map/ppermute | solution.py:44
  58.9 0.8 %finish.1 = f32[64,320]{1,0:T(8,128)} custom-call(f32[48,128]{1,0:T(8,128)S(1)} %get-tuple-element.33.refs_5_.ho, f32[96,128]{1,0:T(8,128)S(1)} %collective-permute-done.7.oa, f32[96,128]{1,0:T(8,128)S(1)} %collective-permute-done.8.ob, f32[48,128]{1,0:T(8,128)S(1)} %collective-permute-done.9.oc, f32[48,128]{1,0:T(8,128)S(1)} %contract.4.hr, ...), custom_call_target="tpu_custom_call" | custom-call | tf_op jit(solution)/shard_map/finish/pallas_call | solution.py:343
Async XLA Ops:
  0.0 4.3 %copy-start = (f32[96,256]{1,0:T(8,128)S(1)}, f32[96,256]{1,0:T(8,128)}, u32[]{:S(2)}) copy-start(f32[96,256]{1,0:T(8,128)} %refs_3_.1) | copy-start | bytes 294916
  1.2 39.8 %collective-permute-start.6 = (f32[1536,128]{1,0:T(8,128)S(1)}, f32[1536,128]{1,0:T(8,128)S(1)}, u32[]{:S(2)}, u32[]{:S(2)}) collective-permute-start(f32[1536,128]{1,0:T(8,128)S(1)} %head.1), channel_id=1, source_target_pairs={{0,16},{16,0},{1,17},{17,1},{2,18},{18,2},{3,19},{19,3},{4,20},{20... | collective-permute-start | bytes 2359304 | tf_op jit(solution)/shard_map/ppermute | solution.py:361
  4.3 7.4 %collective-permute-start.1 = (f32[96,256]{1,0:T(8,128)S(1)}, f32[96,256]{1,0:T(8,128)S(1)}, u32[]{:S(2)}, u32[]{:S(2)}) collective-permute-start(f32[96,256]{1,0:T(8,128)S(1)} %copy-done), channel_id=1, source_target_pairs={{0,2},{1,3},{2,4},{3,5},{4,6},{5,7},{6,8},{7,9},{8,10},{9,11},{10,... | collective-permute-start | bytes 294920 | tf_op jit(solution)/shard_map/ppermute | solution.py:52
  5.8 6.6 %collective-permute-start.4 = (f32[96,256]{1,0:T(8,128)S(1)}, f32[96,256]{1,0:T(8,128)S(1)}, u32[]{:S(2)}, u32[]{:S(2)}) collective-permute-start(f32[96,256]{1,0:T(8,128)S(1)} %copy-done), channel_id=1, source_target_pairs={{0,14},{1,15},{2,0},{3,1},{4,2},{5,3},{6,4},{7,5},{8,6},{9,7},{10,... | collective-permute-start | bytes 294920 | tf_op jit(solution)/shard_map/ppermute | solution.py:52
  9.0 8.0 %collective-permute-start = (f32[96,256]{1,0:T(8,128)S(1)}, f32[96,256]{1,0:T(8,128)S(1)}, u32[]{:S(2)}, u32[]{:S(2)}) collective-permute-start(f32[96,256]{1,0:T(8,128)S(1)} %copy-done), channel_id=1, source_target_pairs={{0,13},{1,4},{2,15},{3,6},{4,1},{5,8},{6,3},{7,10},{8,5},{9,12},{1... | collective-permute-start | bytes 294920 | tf_op jit(solution)/shard_map/ppermute | solution.py:52
  9.4 7.6 %collective-permute-start.3 = (f32[96,256]{1,0:T(8,128)S(1)}, f32[96,256]{1,0:T(8,128)S(1)}, u32[]{:S(2)}, u32[]{:S(2)}) collective-permute-start(f32[96,256]{1,0:T(8,128)S(1)} %copy-done), channel_id=1, source_target_pairs={{0,1},{1,0},{2,3},{3,2},{4,5},{5,4},{6,7},{7,6},{8,9},{9,8},{10,11... | collective-permute-start | bytes 294920 | tf_op jit(solution)/shard_map/ppermute | solution.py:52
  11.7 5.3 %collective-permute-start.2 = (f32[96,256]{1,0:T(8,128)S(1)}, f32[96,256]{1,0:T(8,128)S(1)}, u32[]{:S(2)}, u32[]{:S(2)}) collective-permute-start(f32[96,256]{1,0:T(8,128)S(1)} %collective-permute-done.1.refs_1_), channel_id=1, source_target_pairs={{0,1},{1,0},{2,3},{3,2},{4,5},{5,4},{6,7},{7,6},{8,9},{9,8},{10,11... | collective-permute-start | bytes 294920 | tf_op jit(solution)/shard_map/ppermute | solution.py:52
  12.4 4.7 %collective-permute-start.5 = (f32[96,256]{1,0:T(8,128)S(1)}, f32[96,256]{1,0:T(8,128)S(1)}, u32[]{:S(2)}, u32[]{:S(2)}) collective-permute-start(f32[96,256]{1,0:T(8,128)S(1)} %collective-permute-done.4.refs_5_), channel_id=1, source_target_pairs={{0,1},{1,0},{2,3},{3,2},{4,5},{5,4},{6,7},{7,6},{8,9},{9,8},{10,11... | collective-permute-start | bytes 294920 | tf_op jit(solution)/shard_map/ppermute | solution.py:52
  15.0 2.0 %copy-start.1 = (s32[1,1,3]{2,1,0:T(1,128)S(1)}, s32[1,1,3]{2,1,0:T(1,128)}, u32[]{:S(2)}) copy-start(s32[1,1,3]{2,1,0:T(1,128)} %refs_7_.1) | copy-start | bytes 40
  18.8 24.3 %collective-permute-start.11 = (f32[1024,128]{1,0:T(8,128)S(1)}, f32[1024,128]{1,0:T(8,128)S(1)}, u32[]{:S(2)}, u32[]{:S(2)}) collective-permute-start(f32[1024,128]{1,0:T(8,128)S(1)} %get-tuple-element.36), channel_id=1, source_target_pairs={{0,16},{16,0},{1,17},{17,1},{2,18},{18,2},{3,19},{19,3},{4,20},{20... | collective-permute-start | bytes 1572872 | tf_op jit(solution)/shard_map/ppermute | solution.py:369
  22.2 16.7 %collective-permute-start.10 = (f32[512,128]{1,0:T(8,128)S(1)}, f32[512,128]{1,0:T(8,128)S(1)}, u32[]{:S(2)}, u32[]{:S(2)}) collective-permute-start(f32[512,128]{1,0:T(8,128)S(1)} %get-tuple-element.35), channel_id=1, source_target_pairs={{0,16},{16,0},{1,17},{17,1},{2,18},{18,2},{3,19},{19,3},{4,20},{20... | collective-permute-start | bytes 786440 | tf_op jit(solution)/shard_map/ppermute | solution.py:372
  39.4 14.1 %collective-permute-start.14 = (f32[48,128]{1,0:T(8,128)S(1)}, f32[48,128]{1,0:T(8,128)S(1)}, u32[]{:S(2)}, u32[]{:S(2)}) collective-permute-start(f32[48,128]{1,0:T(8,128)S(1)} %contract.4.hr), channel_id=1, source_target_pairs={{0,16},{1,17},{2,18},{3,19},{4,20},{5,21},{6,22},{7,23},{8,24},{9,... | collective-permute-start | bytes 73736 | tf_op jit(solution)/shard_map/ppermute | solution.py:44
  43.7 13.6 %collective-permute-start.12 = (f32[96,128]{1,0:T(8,128)S(1)}, f32[96,128]{1,0:T(8,128)S(1)}, u32[]{:S(2)}, u32[]{:S(2)}) collective-permute-start(f32[96,128]{1,0:T(8,128)S(1)} %contract.5), channel_id=1, source_target_pairs={{0,1},{1,2},{2,3},{3,4},{4,5},{5,6},{6,7},{7,8},{8,9},{9,10},{10,1... | collective-permute-start | bytes 147464 | tf_op jit(solution)/shard_map/ppermute | solution.py:44
  43.7 13.6 %collective-permute-start.13 = (f32[96,128]{1,0:T(8,128)S(1)}, f32[96,128]{1,0:T(8,128)S(1)}, u32[]{:S(2)}, u32[]{:S(2)}) collective-permute-start(f32[96,128]{1,0:T(8,128)S(1)} %contract.5), channel_id=1, source_target_pairs={{0,17},{1,18},{2,19},{3,20},{4,21},{5,22},{6,23},{7,24},{8,25},{9,... | collective-permute-start | bytes 147464 | tf_op jit(solution)/shard_map/ppermute | solution.py:44
  44.2 13.1 %collective-permute-start.7 = (f32[96,128]{1,0:T(8,128)S(1)}, f32[96,128]{1,0:T(8,128)S(1)}, u32[]{:S(2)}, u32[]{:S(2)}) collective-permute-start(f32[96,128]{1,0:T(8,128)S(1)} %get-tuple-element.34), channel_id=1, source_target_pairs={{0,15},{1,0},{2,1},{3,2},{4,3},{5,4},{6,5},{7,6},{8,7},{9,8},{10,9... | collective-permute-start | bytes 147464 | tf_op jit(solution)/shard_map/ppermute | solution.py:44
  51.8 7.1 %collective-permute-start.8 = (f32[96,128]{1,0:T(8,128)S(1)}, f32[96,128]{1,0:T(8,128)S(1)}, u32[]{:S(2)}, u32[]{:S(2)}) collective-permute-start(f32[96,128]{1,0:T(8,128)S(1)} %get-tuple-element.34), channel_id=1, source_target_pairs={{0,31},{1,16},{2,17},{3,18},{4,19},{5,20},{6,21},{7,22},{8,23},{9,... | collective-permute-start | bytes 147464 | tf_op jit(solution)/shard_map/ppermute | solution.py:44
  53.5 3.8 %collective-permute-start.9 = (f32[48,128]{1,0:T(8,128)S(1)}, f32[48,128]{1,0:T(8,128)S(1)}, u32[]{:S(2)}, u32[]{:S(2)}) collective-permute-start(f32[48,128]{1,0:T(8,128)S(1)} %get-tuple-element.33.refs_5_.ho), channel_id=1, source_target_pairs={{0,16},{1,17},{2,18},{3,19},{4,20},{5,21},{6,22},{7,23},{8,24},{9,... | collective-permute-start | bytes 73736 | tf_op jit(solution)/shard_map/ppermute | solution.py:44
where the time goes:
time: 59.9 us; the launch traced here: 59.7 us
  starting transfers between devices  21.8 us (36%)
  waiting for transfers between devices  21 us (35%)
  Pallas kernels  16.1 us (27%)
  between operations  0.79 us (1%)
    ppermute x1, waiting for transfers between devices, paired(): far_rest = lax.ppermute(far_rest, 'tens', swap)  12.7 us
    ppermute x6, starting transfers between devices, send(): return lax.ppermute(x, ('tens', 'atom'), pairs)  11.4 us
    pallas_call x3, Pallas kernels, prep_t(): pl.pallas_call(body, in_specs=[HB] + [VM] * len(early), out_specs=[VM, VM...  5.89 us
    ppermute x6, waiting for transfers between devices, send(): return lax.ppermute(x, ('tens', 'atom'), pairs)  5.38 us
    ppermute x6, starting transfers between devices, move(): return lax.ppermute(y, 'atom', pairs)  5.13 us
    ppermute x1, starting transfers between devices, paired(): n_far = lax.ppermute(head(n_saved, part), 'tens', swap)  3.06 us
    ppermute x6, waiting for transfers between devices, move(): return lax.ppermute(y, 'atom', pairs)  2.97 us
    pallas_call x3, Pallas kernels, contract(): pl.pallas_call(body, in_specs=[VM] * (len(stretches) + len(flat) + len(af...  2.87 us
  transfers between devices with their start and end apart: 15, of which 5 were waited for; matrix products, arithmetic and copies ran while one was open for 0% of the time, Pallas kernels for 24%

commit v1 on v0

--- a/solution.py
+++ b/solution.py
@@ -325,15 +325,14 @@
     return jnp.concatenate([x[:size], tail], axis=1)[:, :band]
 
 
-def finish(own, rec, orb, band):
-    def body(ho, oa, ob, oc, hr, ra, rb, rc, out):
+def gather(rest, oa, ob, oc, ra, rb, orb, band):
+    def body(h, a, b, c, d, e, out):
         first = lax.axis_index("tens") == 0
-        lower = jnp.where(first, ob[...], oa[...]) + jnp.where(first, ra[...], rb[...])
-        upper = jnp.where(first, oa[...], ob[...]) + jnp.where(first, rb[...], ra[...])
-        x = ho[...] + rc[...]
-        y = oc[...] + hr[...]
-        rest = x.shape[0] * LANES // band
-        x, y = unpack(jnp.where(first, x, y), rest, band), unpack(jnp.where(first, y, x), rest, band)
+        lower = jnp.where(first, b[...], a[...]) + jnp.where(first, d[...], e[...])
+        upper = jnp.where(first, a[...], b[...]) + jnp.where(first, e[...], d[...])
+        x, y = h[...], c[...]
+        size = x.shape[0] * LANES // band
+        x, y = unpack(jnp.where(first, x, y), size, band), unpack(jnp.where(first, y, x), size, band)
         lower, upper = unpack(lower, orb, band), unpack(upper, orb, band)
         zero = jnp.zeros((orb, orb), f32)
         out[...] = (jnp.concatenate([lower, zero, zero], axis=1)
@@ -341,9 +340,24 @@
                     + jnp.concatenate([zero, zero, upper], axis=1))
 
     return pl.pallas_call(
-        body, in_specs=[VM] * 8, out_specs=VM,
-        out_shape=jax.ShapeDtypeStruct((orb, band + 2 * orb), f32), name="finish", compiler_params=limit(8),
-    )(*own, *rec)
+        body, in_specs=[VM] * 6, out_specs=VM, out_shape=vmem((orb, band + 2 * orb), f32),
+        name="gather", compiler_params=limit(8),
+    )(rest, oa, ob, oc, ra, rb)
+
+
+def finish(early, mine, other, orb, band):
+    def body(e, hr, rc, out):
+        first = lax.axis_index("tens") == 0
+        x, y = rc[...], hr[...]
+        size = x.shape[0] * LANES // band
+        x, y = unpack(jnp.where(first, x, y), size, band), unpack(jnp.where(first, y, x), size, band)
+        zero = jnp.zeros((orb, orb), f32)
+        out[...] = e[...] + jnp.concatenate([zero, jnp.concatenate([x, y], axis=0), zero], axis=1)
+
+    return pl.pallas_call(
+        body, in_specs=[VM] * 3, out_specs=VM,
+        out_shape=jax.ShapeDtypeStruct((orb, band + 2 * orb), f32), name="finish", compiler_params=limit(4),
+    )(early, mine, other)
 
 
 def paired(chibar, t_blocks, n_saved, q_list, q_count):
@@ -384,7 +398,8 @@
     rb = send(r_main, lambda t, s: (1 - t, s + 1 - 2 * t))
     r_rest, = contract([far_rest], cross, [near, near], far_rows, band, [rest])
     rc = send(r_rest, lambda t, s: (1 - t, s))
-    return finish((o_rest, oa, ob, oc), (r_rest, ra, rb, rc), orb, band)
+    early_sum = gather(o_rest, oa, ob, oc, ra, rb, orb, band)
+    return finish(early_sum, r_rest, rc, orb, band)
 
 
 def general(chibar, t_blocks, n_saved, q_list, q_count):

time: 59.9 us -> 52.7 us (0.88)
  waiting for transfers between devices: 21 us -> 15.3 us
  starting transfers between devices: 21.8 us -> 20.2 us
    ppermute x1, waiting for transfers between devices: 12.7 us -> 0.01 us  [paired(): far_rest = lax.ppermute(far_rest, 'tens', swap)]
    ppermute x1, waiting for transfers between devices: 0.01 us -> 5.46 us  [paired(): far_main = lax.ppermute(far_main, 'tens', swap)]
    ppermute x6, starting transfers between devices: 11.4 us -> 9.8 us  [send(): return lax.ppermute(x, ('tens', 'atom'), pairs)]
    ppermute x6, waiting for transfers between devices: 5.38 us -> 6.89 us  [send(): return lax.ppermute(x, ('tens', 'atom'), pairs)]
  transfers between devices with their start and end apart: 15 -> 15, of which waited for: 5 -> 6; matrix products, arithmetic and copies ran while one was open for 0% -> 0% of each run, Pallas kernels for 24% -> 27%
where the time goes in v1:
time: 52.7 us; the launch traced here: 52.5 us
  starting transfers between devices  20.2 us (38%)
  Pallas kernels  16.2 us (31%)
  waiting for transfers between devices  15.3 us (29%)
  between operations  0.8 us (2%)
    ppermute x6, starting transfers between devices, send(): return lax.ppermute(x, ('tens', 'atom'), pairs)  9.8 us
    ppermute x6, waiting for transfers between devices, send(): return lax.ppermute(x, ('tens', 'atom'), pairs)  6.89 us
    pallas_call x3, Pallas kernels, prep_t(): pl.pallas_call(body, in_specs=[HB] + [VM] * len(early), out_specs=[VM, VM...  5.89 us
    ppermute x1, waiting for transfers between devices, paired(): far_main = lax.ppermute(far_main, 'tens', swap)  5.46 us
    ppermute x6, starting transfers between devices, move(): return lax.ppermute(y, 'atom', pairs)  5.13 us
    ppermute x1, starting transfers between devices, paired(): n_far = lax.ppermute(head(n_saved, part), 'tens', swap)  3.06 us
    ppermute x6, waiting for transfers between devices, move(): return lax.ppermute(y, 'atom', pairs)  2.97 us
    pallas_call x3, Pallas kernels, contract(): pl.pallas_call(body, in_specs=[VM] * (len(stretches) + len(flat) + len(af...  2.86 us
  transfers between devices with their start and end apart: 15, of which 6 were waited for; matrix products, arithmetic and copies ran while one was open for 0% of the time, Pallas kernels for 27%

profile of v1, /device:TPU:0, one launch (start us, length us, event | category | flops | bytes accessed | tf_op | source)
XLA Modules:
  0.0 52.5 jit_solution(1847603583749490582)
XLA Ops:
  0.0 0.0 copy-start
  0.0 1.2 %head.1 = f32[1536,128]{1,0:T(8,128)S(1)} custom-call(f32[48,12288]{1,0:T(8,128)} %src.9), custom_call_target="tpu_custom_call" | custom-call | tf_op jit(solution)/shard_map/head/pallas_call | solution.py:108
  1.2 3.1 %collective-permute-start.6 = (f32[1536,128]{1,0:T(8,128)S(1)}, f32[1536,128]{1,0:T(8,128)S(1)}, u32[]{:S(2)}, u32[]{:S(2)}) collective-permute-start(f32[1536,128]{1,0:T(8,128)S(1)} %head.1), channel_id=1, source_target_pairs={{0,16},{16,0},{1,17},{17,1},{2,18},{18,2},{3,19},{19,3},{4,20},{20... | collective-permute-start | bytes 2359304 | tf_op jit(solution)/shard_map/ppermute | solution.py:375
  4.3 0.0 copy-done
  4.3 1.5 %collective-permute-start.1 = (f32[96,256]{1,0:T(8,128)S(1)}, f32[96,256]{1,0:T(8,128)S(1)}, u32[]{:S(2)}, u32[]{:S(2)}) collective-permute-start(f32[96,256]{1,0:T(8,128)S(1)} %copy-done), channel_id=1, source_target_pairs={{0,2},{1,3},{2,4},{3,5},{4,6},{5,7},{6,8},{7,9},{8,10},{9,11},{10,... | collective-permute-start | bytes 294920 | tf_op jit(solution)/shard_map/ppermute | solution.py:52
  5.8 3.2 %collective-permute-start.4 = (f32[96,256]{1,0:T(8,128)S(1)}, f32[96,256]{1,0:T(8,128)S(1)}, u32[]{:S(2)}, u32[]{:S(2)}) collective-permute-start(f32[96,256]{1,0:T(8,128)S(1)} %copy-done), channel_id=1, source_target_pairs={{0,14},{1,15},{2,0},{3,1},{4,2},{5,3},{6,4},{7,5},{8,6},{9,7},{10,... | collective-permute-start | bytes 294920 | tf_op jit(solution)/shard_map/ppermute | solution.py:52
  9.0 0.4 collective-permute-start
  9.4 0.0 collective-permute-start.3
  9.4 2.3 %collective-permute-done.1.refs_1_ = f32[96,256]{1,0:T(8,128)S(1)} collective-permute-done((f32[96,256]{1,0:T(8,128)S(1)}, f32[96,256]{1,0:T(8,128)S(1)}, u32[]{:S(2)}, u32[]{:S(2)}) %collective-permute-start.1) | collective-permute-done | bytes 98336 | tf_op jit(solution)/shard_map/ppermute | solution.py:52
  11.7 0.0 collective-permute-start.2
  11.7 0.7 %collective-permute-done.4.refs_5_ = f32[96,256]{1,0:T(8,128)S(1)} collective-permute-done((f32[96,256]{1,0:T(8,128)S(1)}, f32[96,256]{1,0:T(8,128)S(1)}, u32[]{:S(2)}, u32[]{:S(2)}) %collective-permute-start.4) | collective-permute-done | bytes 98336 | tf_op jit(solution)/shard_map/ppermute | solution.py:52
  12.4 0.0 collective-permute-start.5
  13.1 2.0 %prep_t.4 = (bf16[384,2048]{1,0:T(8,128)(2,1)S(1)}, bf16[384,2048]{1,0:T(8,128)(2,1)S(1)}) custom-call(f32[384,6144]{1,0:T(8,128)} %src.7), custom_call_target="tpu_custom_call" | custom-call | tf_op jit(solution)/shard_map/prep_t/pallas_call | solution.py:87
  15.0 0.0 copy-start.1
  15.0 2.0 %prep_t.3 = (bf16[384,2048]{1,0:T(8,128)(2,1)S(1)}, bf16[384,2048]{1,0:T(8,128)(2,1)S(1)}) custom-call(f32[384,6144]{1,0:T(8,128)} %src.7, s32[1,1]{1,0:T(1,128)S(6)} %copy.6.refs_8_.refs_0_), custom_call_target="tpu_custom_call" | custom-call | tf_op jit(solution)/shard_map/prep_t/pallas_call | solution.py:87
  17.0 0.0 collective-permute-done.refs_0_
  17.0 0.0 collective-permute-done.3.refs_4_
  17.0 0.0 collective-permute-done.2.refs_2_
  17.0 0.0 collective-permute-done.5.refs_6_
  17.1 0.0 copy-done.1
  17.1 0.2 select.1.c
  17.3 1.5 %multiply.2 = (f32[1024,128]{1,0:T(8,128)S(1)}, f32[2048,128]{1,0:T(8,128)S(1)}) custom-call(bf16[192,384]{1,0:T(8,128)(2,1)S(1)} %select.1.c, bf16[384,2048]{1,0:T(8,128)(2,1)S(1)} %get-tuple-element.21.refs_0_, bf16[384,2048]{1,0:T(8,128)(2,1)S(1)} %get-tuple-element.22.refs_1_, bf16[384,2048]{1,0:T(8,128)(2,1)S(1)} %get-tuple-element.23.refs_2_, ...), custom_call_target="tpu_custom_call" | custom-call | tf_op jit(solution)/shard_map/multiply/pallas_call | solution.py:244
  18.8 0.6 %collective-permute-start.10 = (f32[1024,128]{1,0:T(8,128)S(1)}, f32[1024,128]{1,0:T(8,128)S(1)}, u32[]{:S(2)}, u32[]{:S(2)}) collective-permute-start(f32[1024,128]{1,0:T(8,128)S(1)} %get-tuple-element.35), channel_id=1, source_target_pairs={{0,16},{16,0},{1,17},{17,1},{2,18},{18,2},{3,19},{19,3},{4,20},{20... | collective-permute-start | bytes 1572872 | tf_op jit(solution)/shard_map/ppermute | solution.py:383
  19.4 2.0 %prep_t.5 = (bf16[384,2048]{1,0:T(8,128)(2,1)S(1)}, bf16[384,2048]{1,0:T(8,128)(2,1)S(1)}) custom-call(f32[384,6144]{1,0:T(8,128)} %src.7), custom_call_target="tpu_custom_call" | custom-call | tf_op jit(solution)/shard_map/prep_t/pallas_call | solution.py:87
  21.3 0.8 %multiply.3 = (f32[512,128]{1,0:T(8,128)S(1)}, f32[1024,128]{1,0:T(8,128)S(1)}) custom-call(bf16[192,384]{1,0:T(8,128)(2,1)S(1)} %select.1.c, bf16[384,2048]{1,0:T(8,128)(2,1)S(1)} %get-tuple-element.26.refs_0_, bf16[384,2048]{1,0:T(8,128)(2,1)S(1)} %get-tuple-element.27.refs_1_), custom_call_target="tpu_custom_call" | custom-call | tf_op jit(solution)/shard_map/multiply/pallas_call | solution.py:244
  22.2 1.6 %collective-permute-start.13 = (f32[512,128]{1,0:T(8,128)S(1)}, f32[512,128]{1,0:T(8,128)S(1)}, u32[]{:S(2)}, u32[]{:S(2)}) collective-permute-start(f32[512,128]{1,0:T(8,128)S(1)} %get-tuple-element.36), channel_id=1, source_target_pairs={{0,16},{16,0},{1,17},{17,1},{2,18},{18,2},{3,19},{19,3},{4,20},{20... | collective-permute-start | bytes 786440 | tf_op jit(solution)/shard_map/ppermute | solution.py:386
  23.7 2.4 %prep_n.1 = (bf16[3072,256]{1,0:T(8,128)(2,1)S(1)}, bf16[3072,256]{1,0:T(8,128)(2,1)S(1)}) custom-call(f32[48,12288]{1,0:T(8,128)} %src.9), custom_call_target="tpu_custom_call" | custom-call | tf_op jit(solution)/shard_map/prep_n/pallas_call | solution.py:155
  26.2 0.0 collective-permute-done.6.src
  26.2 0.4 prep_far.1
  26.5 1.7 %contract.3 = (f32[96,128]{1,0:T(8,128)S(1)}, f32[48,128]{1,0:T(8,128)S(1)}) custom-call(f32[2048,128]{1,0:T(8,128)S(1)} %get-tuple-element.25.refs_0_, f32[1024,128]{1,0:T(8,128)S(1)} %get-tuple-element.28.refs_1_, bf16[3072,256]{1,0:T(8,128)(2,1)S(1)} %get-tuple-element.29.refs_2_.refs_1_.refs_3_, ...), custom_call_target="tpu_custom_call" | custom-call | tf_op jit(solution)/shard_map/contract/pallas_call | solution.py:315
  28.2 5.5 %collective-permute-done.10.refs_0_ = f32[1024,128]{1,0:T(8,128)S(1)} collective-permute-done((f32[1024,128]{1,0:T(8,128)S(1)}, f32[1024,128]{1,0:T(8,128)S(1)}, u32[]{:S(2)}, u32[]{:S(2)}) %collective-permute-start.10) | collective-permute-done | bytes 524320 | tf_op jit(solution)/shard_map/ppermute | solution.py:383
  33.7 0.6 %contract.4 = f32[96,128]{1,0:T(8,128)S(1)} custom-call(f32[1024,128]{1,0:T(8,128)S(1)} %collective-permute-done.10.refs_0_, bf16[3072,256]{1,0:T(8,128)(2,1)S(1)} %get-tuple-element.29.refs_2_.refs_1_.refs_3_, bf16[3072,256]{1,0:T(8,128)(2,1)S(1)} %get-tuple-element.30.refs_3_.refs_2_.refs_4_, ...), custom_call_target="tpu_custom_call" | custom-call | tf_op jit(solution)/shard_map/contract/pallas_call | solution.py:315
  34.3 0.0 collective-permute-start.11
  34.3 2.4 %collective-permute-start.12 = (f32[96,128]{1,0:T(8,128)S(1)}, f32[96,128]{1,0:T(8,128)S(1)}, u32[]{:S(2)}, u32[]{:S(2)}) collective-permute-start(f32[96,128]{1,0:T(8,128)S(1)} %contract.4), channel_id=1, source_target_pairs={{0,17},{1,18},{2,19},{3,20},{4,21},{5,22},{6,23},{7,24},{8,25},{9,... | collective-permute-start | bytes 147464 | tf_op jit(solution)/shard_map/ppermute | solution.py:44
  36.7 5.8 %collective-permute-start.7 = (f32[96,128]{1,0:T(8,128)S(1)}, f32[96,128]{1,0:T(8,128)S(1)}, u32[]{:S(2)}, u32[]{:S(2)}) collective-permute-start(f32[96,128]{1,0:T(8,128)S(1)} %get-tuple-element.34), channel_id=1, source_target_pairs={{0,15},{1,0},{2,1},{3,2},{4,3},{5,4},{6,5},{7,6},{8,7},{9,8},{10,9... | collective-permute-start | bytes 147464 | tf_op jit(solution)/shard_map/ppermute | solution.py:44
  42.4 1.6 %collective-permute-start.8 = (f32[96,128]{1,0:T(8,128)S(1)}, f32[96,128]{1,0:T(8,128)S(1)}, u32[]{:S(2)}, u32[]{:S(2)}) collective-permute-start(f32[96,128]{1,0:T(8,128)S(1)} %get-tuple-element.34), channel_id=1, source_target_pairs={{0,31},{1,16},{2,17},{3,18},{4,19},{5,20},{6,21},{7,22},{8,23},{9,... | collective-permute-start | bytes 147464 | tf_op jit(solution)/shard_map/ppermute | solution.py:44
  44.1 0.0 collective-permute-done.13.refs_0_
  44.1 0.0 collective-permute-start.9
  44.1 0.6 %contract.5.hr = f32[48,128]{1,0:T(8,128)S(1)} custom-call(f32[512,128]{1,0:T(8,128)S(1)} %collective-permute-done.13.refs_0_, bf16[3072,256]{1,0:T(8,128)(2,1)S(1)} %get-tuple-element.29.refs_2_.refs_1_.refs_3_, bf16[3072,256]{1,0:T(8,128)(2,1)S(1)} %get-tuple-element.30.refs_3_.refs_2_.refs_4_, ...), custom_call_target="tpu_custom_call" | custom-call | tf_op jit(solution)/shard_map/contract/pallas_call | solution.py:315
  44.7 3.2 %collective-permute-done.9.c = f32[48,128]{1,0:T(8,128)S(1)} collective-permute-done((f32[48,128]{1,0:T(8,128)S(1)}, f32[48,128]{1,0:T(8,128)S(1)}, u32[]{:S(2)}, u32[]{:S(2)}) %collective-permute-start.9) | collective-permute-done | bytes 24608 | tf_op jit(solution)/shard_map/ppermute | solution.py:44
  47.9 0.0 collective-permute-start.14
  47.9 0.0 collective-permute-done.11.d
  47.9 0.0 collective-permute-done.12.e
  47.9 0.0 collective-permute-done.7.a
  47.9 1.6 %collective-permute-done.8.b = f32[96,128]{1,0:T(8,128)S(1)} collective-permute-done((f32[96,128]{1,0:T(8,128)S(1)}, f32[96,128]{1,0:T(8,128)S(1)}, u32[]{:S(2)}, u32[]{:S(2)}) %collective-permute-start.8) | collective-permute-done | bytes 49184 | tf_op jit(solution)/shard_map/ppermute | solution.py:44
  49.5 0.1 gather.1.e
  49.7 2.0 %collective-permute-done.14.rc = f32[48,128]{1,0:T(8,128)S(1)} collective-permute-done((f32[48,128]{1,0:T(8,128)S(1)}, f32[48,128]{1,0:T(8,128)S(1)}, u32[]{:S(2)}, u32[]{:S(2)}) %collective-permute-start.14) | collective-permute-done | bytes 24608 | tf_op jit(solution)/shard_map/ppermute | solution.py:44
  51.7 0.8 %finish.1 = f32[64,320]{1,0:T(8,128)} custom-call(f32[64,320]{1,0:T(8,128)S(1)} %gather.1.e, f32[48,128]{1,0:T(8,128)S(1)} %contract.5.hr, f32[48,128]{1,0:T(8,128)S(1)} %collective-permute-done.14.rc), custom_call_target="tpu_custom_call" | custom-call | tf_op jit(solution)/shard_map/finish/pallas_call | solution.py:357
Async XLA Ops:
  0.0 4.3 %copy-start = (f32[96,256]{1,0:T(8,128)S(1)}, f32[96,256]{1,0:T(8,128)}, u32[]{:S(2)}) copy-start(f32[96,256]{1,0:T(8,128)} %refs_3_.1) | copy-start | bytes 294916
  1.2 24.9 %collective-permute-start.6 = (f32[1536,128]{1,0:T(8,128)S(1)}, f32[1536,128]{1,0:T(8,128)S(1)}, u32[]{:S(2)}, u32[]{:S(2)}) collective-permute-start(f32[1536,128]{1,0:T(8,128)S(1)} %head.1), channel_id=1, source_target_pairs={{0,16},{16,0},{1,17},{17,1},{2,18},{18,2},{3,19},{19,3},{4,20},{20... | collective-permute-start | bytes 2359304 | tf_op jit(solution)/shard_map/ppermute | solution.py:375
  4.3 7.4 %collective-permute-start.1 = (f32[96,256]{1,0:T(8,128)S(1)}, f32[96,256]{1,0:T(8,128)S(1)}, u32[]{:S(2)}, u32[]{:S(2)}) collective-permute-start(f32[96,256]{1,0:T(8,128)S(1)} %copy-done), channel_id=1, source_target_pairs={{0,2},{1,3},{2,4},{3,5},{4,6},{5,7},{6,8},{7,9},{8,10},{9,11},{10,... | collective-permute-start | bytes 294920 | tf_op jit(solution)/shard_map/ppermute | solution.py:52
  5.8 6.6 %collective-permute-start.4 = (f32[96,256]{1,0:T(8,128)S(1)}, f32[96,256]{1,0:T(8,128)S(1)}, u32[]{:S(2)}, u32[]{:S(2)}) collective-permute-start(f32[96,256]{1,0:T(8,128)S(1)} %copy-done), channel_id=1, source_target_pairs={{0,14},{1,15},{2,0},{3,1},{4,2},{5,3},{6,4},{7,5},{8,6},{9,7},{10,... | collective-permute-start | bytes 294920 | tf_op jit(solution)/shard_map/ppermute | solution.py:52
  9.0 8.0 %collective-permute-start = (f32[96,256]{1,0:T(8,128)S(1)}, f32[96,256]{1,0:T(8,128)S(1)}, u32[]{:S(2)}, u32[]{:S(2)}) collective-permute-start(f32[96,256]{1,0:T(8,128)S(1)} %copy-done), channel_id=1, source_target_pairs={{0,13},{1,4},{2,15},{3,6},{4,1},{5,8},{6,3},{7,10},{8,5},{9,12},{1... | collective-permute-start | bytes 294920 | tf_op jit(solution)/shard_map/ppermute | solution.py:52
  9.4 7.6 %collective-permute-start.3 = (f32[96,256]{1,0:T(8,128)S(1)}, f32[96,256]{1,0:T(8,128)S(1)}, u32[]{:S(2)}, u32[]{:S(2)}) collective-permute-start(f32[96,256]{1,0:T(8,128)S(1)} %copy-done), channel_id=1, source_target_pairs={{0,1},{1,0},{2,3},{3,2},{4,5},{5,4},{6,7},{7,6},{8,9},{9,8},{10,11... | collective-permute-start | bytes 294920 | tf_op jit(solution)/shard_map/ppermute | solution.py:52
  11.7 5.3 %collective-permute-start.2 = (f32[96,256]{1,0:T(8,128)S(1)}, f32[96,256]{1,0:T(8,128)S(1)}, u32[]{:S(2)}, u32[]{:S(2)}) collective-permute-start(f32[96,256]{1,0:T(8,128)S(1)} %collective-permute-done.1.refs_1_), channel_id=1, source_target_pairs={{0,1},{1,0},{2,3},{3,2},{4,5},{5,4},{6,7},{7,6},{8,9},{9,8},{10,11... | collective-permute-start | bytes 294920 | tf_op jit(solution)/shard_map/ppermute | solution.py:52
  12.4 4.7 %collective-permute-start.5 = (f32[96,256]{1,0:T(8,128)S(1)}, f32[96,256]{1,0:T(8,128)S(1)}, u32[]{:S(2)}, u32[]{:S(2)}) collective-permute-start(f32[96,256]{1,0:T(8,128)S(1)} %collective-permute-done.4.refs_5_), channel_id=1, source_target_pairs={{0,1},{1,0},{2,3},{3,2},{4,5},{5,4},{6,7},{7,6},{8,9},{9,8},{10,11... | collective-permute-start | bytes 294920 | tf_op jit(solution)/shard_map/ppermute | solution.py:52
  15.0 2.0 %copy-start.1 = (s32[1,1,3]{2,1,0:T(1,128)S(1)}, s32[1,1,3]{2,1,0:T(1,128)}, u32[]{:S(2)}) copy-start(s32[1,1,3]{2,1,0:T(1,128)} %refs_7_.1) | copy-start | bytes 40
  18.8 14.9 %collective-permute-start.10 = (f32[1024,128]{1,0:T(8,128)S(1)}, f32[1024,128]{1,0:T(8,128)S(1)}, u32[]{:S(2)}, u32[]{:S(2)}) collective-permute-start(f32[1024,128]{1,0:T(8,128)S(1)} %get-tuple-element.35), channel_id=1, source_target_pairs={{0,16},{16,0},{1,17},{17,1},{2,18},{18,2},{3,19},{19,3},{4,20},{20... | collective-permute-start | bytes 1572872 | tf_op jit(solution)/shard_map/ppermute | solution.py:383
  22.2 21.9 %collective-permute-start.13 = (f32[512,128]{1,0:T(8,128)S(1)}, f32[512,128]{1,0:T(8,128)S(1)}, u32[]{:S(2)}, u32[]{:S(2)}) collective-permute-start(f32[512,128]{1,0:T(8,128)S(1)} %get-tuple-element.36), channel_id=1, source_target_pairs={{0,16},{16,0},{1,17},{17,1},{2,18},{18,2},{3,19},{19,3},{4,20},{20... | collective-permute-start | bytes 786440 | tf_op jit(solution)/shard_map/ppermute | solution.py:386
  34.3 13.6 %collective-permute-start.11 = (f32[96,128]{1,0:T(8,128)S(1)}, f32[96,128]{1,0:T(8,128)S(1)}, u32[]{:S(2)}, u32[]{:S(2)}) collective-permute-start(f32[96,128]{1,0:T(8,128)S(1)} %contract.4), channel_id=1, source_target_pairs={{0,1},{1,2},{2,3},{3,4},{4,5},{5,6},{6,7},{7,8},{8,9},{9,10},{10,1... | collective-permute-start | bytes 147464 | tf_op jit(solution)/shard_map/ppermute | solution.py:44
  34.3 13.6 %collective-permute-start.12 = (f32[96,128]{1,0:T(8,128)S(1)}, f32[96,128]{1,0:T(8,128)S(1)}, u32[]{:S(2)}, u32[]{:S(2)}) collective-permute-start(f32[96,128]{1,0:T(8,128)S(1)} %contract.4), channel_id=1, source_target_pairs={{0,17},{1,18},{2,19},{3,20},{4,21},{5,22},{6,23},{7,24},{8,25},{9,... | collective-permute-start | bytes 147464 | tf_op jit(solution)/shard_map/ppermute | solution.py:44
  36.7 11.3 %collective-permute-start.7 = (f32[96,128]{1,0:T(8,128)S(1)}, f32[96,128]{1,0:T(8,128)S(1)}, u32[]{:S(2)}, u32[]{:S(2)}) collective-permute-start(f32[96,128]{1,0:T(8,128)S(1)} %get-tuple-element.34), channel_id=1, source_target_pairs={{0,15},{1,0},{2,1},{3,2},{4,3},{5,4},{6,5},{7,6},{8,7},{9,8},{10,9... | collective-permute-start | bytes 147464 | tf_op jit(solution)/shard_map/ppermute | solution.py:44
  42.4 7.1 %collective-permute-start.8 = (f32[96,128]{1,0:T(8,128)S(1)}, f32[96,128]{1,0:T(8,128)S(1)}, u32[]{:S(2)}, u32[]{:S(2)}) collective-permute-start(f32[96,128]{1,0:T(8,128)S(1)} %get-tuple-element.34), channel_id=1, source_target_pairs={{0,31},{1,16},{2,17},{3,18},{4,19},{5,20},{6,21},{7,22},{8,23},{9,... | collective-permute-start | bytes 147464 | tf_op jit(solution)/shard_map/ppermute | solution.py:44
  44.1 3.8 %collective-permute-start.9 = (f32[48,128]{1,0:T(8,128)S(1)}, f32[48,128]{1,0:T(8,128)S(1)}, u32[]{:S(2)}, u32[]{:S(2)}) collective-permute-start(f32[48,128]{1,0:T(8,128)S(1)} %get-tuple-element.33.refs_5_.h), channel_id=1, source_target_pairs={{0,16},{1,17},{2,18},{3,19},{4,20},{5,21},{6,22},{7,23},{8,24},{9,... | collective-permute-start | bytes 73736 | tf_op jit(solution)/shard_map/ppermute | solution.py:44
  47.9 3.8 %collective-permute-start.14 = (f32[48,128]{1,0:T(8,128)S(1)}, f32[48,128]{1,0:T(8,128)S(1)}, u32[]{:S(2)}, u32[]{:S(2)}) collective-permute-start(f32[48,128]{1,0:T(8,128)S(1)} %contract.5.hr), channel_id=1, source_target_pairs={{0,16},{1,17},{2,18},{3,19},{4,20},{5,21},{6,22},{7,23},{8,24},{9,... | collective-permute-start | bytes 73736 | tf_op jit(solution)/shard_map/ppermute | solution.py:44

commit v2 on v0

--- a/solution.py
+++ b/solution.py
@@ -96,18 +96,21 @@
     tiles = x.shape[1] // LANES
     rows = 2 * SUBL
 
-    def body(src, out, buf, sem):
-        copy = pltpu.make_async_copy(src.at[pl.ds(0, rows)], buf, sem)
-        copy.start()
-        copy.wait()
+    def body(src, out, buf, sems):
+        copies = [pltpu.make_async_copy(src.at[pl.ds(i * SUBL, SUBL)], buf.at[pl.ds(i * SUBL, SUBL)], sems.at[i])
+                  for i in range(2)]
+        for copy in copies:
+            copy.start()
+        copies[0].wait()
         for c in range(tiles):
-            at = pl.ds(c * LANES, LANES)
-            out[pl.ds(c * SUBL, SUBL), :] = buf[:SUBL, at]
-            out[pl.ds(tiles * SUBL + c * part, part), :] = buf[SUBL:SUBL + part, at]
+            out[pl.ds(c * SUBL, SUBL), :] = buf[:SUBL, pl.ds(c * LANES, LANES)]
+        copies[1].wait()
+        for c in range(tiles):
+            out[pl.ds(tiles * SUBL + c * part, part), :] = buf[SUBL:SUBL + part, pl.ds(c * LANES, LANES)]
 
     return pl.pallas_call(
         body, in_specs=[HB], out_specs=VM, out_shape=vmem((tiles * (SUBL + part), LANES), x.dtype),
-        scratch_shapes=[pltpu.VMEM((rows, x.shape[1]), f32), pltpu.SemaphoreType.DMA],
+        scratch_shapes=[pltpu.VMEM((rows, x.shape[1]), f32), pltpu.SemaphoreType.DMA((2,))],
         name="head", compiler_params=limit(4),
     )(x)
 

time: 59.9 us -> 59.9 us (level)
  no operation moved by 1% of the time
where the time goes in v2:
time: 59.9 us; the launch traced here: 59.7 us
  starting transfers between devices  21.8 us (36%)
  waiting for transfers between devices  21 us (35%)
  Pallas kernels  16 us (27%)
  between operations  0.79 us (1%)
    ppermute x1, waiting for transfers between devices, paired(): far_rest = lax.ppermute(far_rest, 'tens', swap)  12.7 us
    ppermute x6, starting transfers between devices, send(): return lax.ppermute(x, ('tens', 'atom'), pairs)  11.4 us
    pallas_call x3, Pallas kernels, prep_t(): pl.pallas_call(body, in_specs=[HB] + [VM] * len(early), out_specs=[VM, VM...  5.89 us
    ppermute x6, waiting for transfers between devices, send(): return lax.ppermute(x, ('tens', 'atom'), pairs)  5.4 us
    ppermute x6, starting transfers between devices, move(): return lax.ppermute(y, 'atom', pairs)  5.13 us
    ppermute x1, starting transfers between devices, paired(): n_far = lax.ppermute(head(n_saved, part), 'tens', swap)  3.06 us
    ppermute x6, waiting for transfers between devices, move(): return lax.ppermute(y, 'atom', pairs)  2.97 us
    pallas_call x3, Pallas kernels, contract(): pl.pallas_call(body, in_specs=[VM] * (len(stretches) + len(flat) + len(af...  2.87 us
  transfers between devices with their start and end apart: 15, of which 5 were waited for; matrix products, arithmetic and copies ran while one was open for 0% of the time, Pallas kernels for 24%

profile of v2, /device:TPU:0, one launch (start us, length us, event | category | flops | bytes accessed | tf_op | source)
XLA Modules:
  0.0 59.7 jit_solution(4813436347007549563)
XLA Ops:
  0.0 0.0 copy-start
  0.0 1.2 %head.1 = f32[1536,128]{1,0:T(8,128)S(1)} custom-call(f32[48,12288]{1,0:T(8,128)} %src.9), custom_call_target="tpu_custom_call" | custom-call | tf_op jit(solution)/shard_map/head/pallas_call | solution.py:111
  1.2 3.1 %collective-permute-start.6 = (f32[1536,128]{1,0:T(8,128)S(1)}, f32[1536,128]{1,0:T(8,128)S(1)}, u32[]{:S(2)}, u32[]{:S(2)}) collective-permute-start(f32[1536,128]{1,0:T(8,128)S(1)} %head.1), channel_id=1, source_target_pairs={{0,16},{16,0},{1,17},{17,1},{2,18},{18,2},{3,19},{19,3},{4,20},{20... | collective-permute-start | bytes 2359304 | tf_op jit(solution)/shard_map/ppermute | solution.py:364
  4.3 0.0 copy-done
  4.3 1.5 %collective-permute-start.1 = (f32[96,256]{1,0:T(8,128)S(1)}, f32[96,256]{1,0:T(8,128)S(1)}, u32[]{:S(2)}, u32[]{:S(2)}) collective-permute-start(f32[96,256]{1,0:T(8,128)S(1)} %copy-done), channel_id=1, source_target_pairs={{0,2},{1,3},{2,4},{3,5},{4,6},{5,7},{6,8},{7,9},{8,10},{9,11},{10,... | collective-permute-start | bytes 294920 | tf_op jit(solution)/shard_map/ppermute | solution.py:52
  5.8 3.2 %collective-permute-start.4 = (f32[96,256]{1,0:T(8,128)S(1)}, f32[96,256]{1,0:T(8,128)S(1)}, u32[]{:S(2)}, u32[]{:S(2)}) collective-permute-start(f32[96,256]{1,0:T(8,128)S(1)} %copy-done), channel_id=1, source_target_pairs={{0,14},{1,15},{2,0},{3,1},{4,2},{5,3},{6,4},{7,5},{8,6},{9,7},{10,... | collective-permute-start | bytes 294920 | tf_op jit(solution)/shard_map/ppermute | solution.py:52
  9.0 0.4 collective-permute-start
  9.4 0.0 collective-permute-start.3
  9.4 2.3 %collective-permute-done.1.refs_1_ = f32[96,256]{1,0:T(8,128)S(1)} collective-permute-done((f32[96,256]{1,0:T(8,128)S(1)}, f32[96,256]{1,0:T(8,128)S(1)}, u32[]{:S(2)}, u32[]{:S(2)}) %collective-permute-start.1) | collective-permute-done | bytes 98336 | tf_op jit(solution)/shard_map/ppermute | solution.py:52
  11.7 0.0 collective-permute-start.2
  11.7 0.7 %collective-permute-done.4.refs_5_ = f32[96,256]{1,0:T(8,128)S(1)} collective-permute-done((f32[96,256]{1,0:T(8,128)S(1)}, f32[96,256]{1,0:T(8,128)S(1)}, u32[]{:S(2)}, u32[]{:S(2)}) %collective-permute-start.4) | collective-permute-done | bytes 98336 | tf_op jit(solution)/shard_map/ppermute | solution.py:52
  12.4 0.0 collective-permute-start.5
  13.0 2.0 %prep_t.4 = (bf16[384,2048]{1,0:T(8,128)(2,1)S(1)}, bf16[384,2048]{1,0:T(8,128)(2,1)S(1)}) custom-call(f32[384,6144]{1,0:T(8,128)} %src.7), custom_call_target="tpu_custom_call" | custom-call | tf_op jit(solution)/shard_map/prep_t/pallas_call | solution.py:87
  15.0 0.0 copy-start.1
  15.0 2.0 %prep_t.3 = (bf16[384,2048]{1,0:T(8,128)(2,1)S(1)}, bf16[384,2048]{1,0:T(8,128)(2,1)S(1)}) custom-call(f32[384,6144]{1,0:T(8,128)} %src.7, s32[1,1]{1,0:T(1,128)S(6)} %copy.6.refs_8_.refs_0_), custom_call_target="tpu_custom_call" | custom-call | tf_op jit(solution)/shard_map/prep_t/pallas_call | solution.py:87
  17.0 0.0 collective-permute-done.refs_0_
  17.0 0.0 collective-permute-done.3.refs_4_
  17.0 0.0 collective-permute-done.2.refs_2_
  17.0 0.0 collective-permute-done.5.refs_6_
  17.0 0.0 copy-done.1
  17.0 0.2 select.1.c
  17.3 1.5 %multiply.2 = (f32[1024,128]{1,0:T(8,128)S(1)}, f32[2048,128]{1,0:T(8,128)S(1)}) custom-call(bf16[192,384]{1,0:T(8,128)(2,1)S(1)} %select.1.c, bf16[384,2048]{1,0:T(8,128)(2,1)S(1)} %get-tuple-element.21.refs_0_, bf16[384,2048]{1,0:T(8,128)(2,1)S(1)} %get-tuple-element.22.refs_1_, bf16[384,2048]{1,0:T(8,128)(2,1)S(1)} %get-tuple-element.23.refs_2_, ...), custom_call_target="tpu_custom_call" | custom-call | tf_op jit(solution)/shard_map/multiply/pallas_call | solution.py:247
  18.8 0.6 collective-permute-start.11
  19.3 2.0 %prep_t.5 = (bf16[384,2048]{1,0:T(8,128)(2,1)S(1)}, bf16[384,2048]{1,0:T(8,128)(2,1)S(1)}) custom-call(f32[384,6144]{1,0:T(8,128)} %src.7), custom_call_target="tpu_custom_call" | custom-call | tf_op jit(solution)/shard_map/prep_t/pallas_call | solution.py:87
  21.3 0.8 %multiply.3 = (f32[512,128]{1,0:T(8,128)S(1)}, f32[1024,128]{1,0:T(8,128)S(1)}) custom-call(bf16[192,384]{1,0:T(8,128)(2,1)S(1)} %select.1.c, bf16[384,2048]{1,0:T(8,128)(2,1)S(1)} %get-tuple-element.26.refs_0_, bf16[384,2048]{1,0:T(8,128)(2,1)S(1)} %get-tuple-element.27.refs_1_), custom_call_target="tpu_custom_call" | custom-call | tf_op jit(solution)/shard_map/multiply/pallas_call | solution.py:247
  22.1 1.6 %collective-permute-start.10 = (f32[512,128]{1,0:T(8,128)S(1)}, f32[512,128]{1,0:T(8,128)S(1)}, u32[]{:S(2)}, u32[]{:S(2)}) collective-permute-start(f32[512,128]{1,0:T(8,128)S(1)} %get-tuple-element.35), channel_id=1, source_target_pairs={{0,16},{16,0},{1,17},{17,1},{2,18},{18,2},{3,19},{19,3},{4,20},{20... | collective-permute-start | bytes 786440 | tf_op jit(solution)/shard_map/ppermute | solution.py:375
  23.7 2.4 %prep_n.1 = (bf16[3072,256]{1,0:T(8,128)(2,1)S(1)}, bf16[3072,256]{1,0:T(8,128)(2,1)S(1)}) custom-call(f32[48,12288]{1,0:T(8,128)} %src.9), custom_call_target="tpu_custom_call" | custom-call | tf_op jit(solution)/shard_map/prep_n/pallas_call | solution.py:158
  26.1 12.7 %collective-permute-done.10.refs_0_ = f32[512,128]{1,0:T(8,128)S(1)} collective-permute-done((f32[512,128]{1,0:T(8,128)S(1)}, f32[512,128]{1,0:T(8,128)S(1)}, u32[]{:S(2)}, u32[]{:S(2)}) %collective-permute-start.10) | collective-permute-done | bytes 262176 | tf_op jit(solution)/shard_map/ppermute | solution.py:375
  38.8 0.6 contract.4.hr
  39.4 1.6 %collective-permute-start.14 = (f32[48,128]{1,0:T(8,128)S(1)}, f32[48,128]{1,0:T(8,128)S(1)}, u32[]{:S(2)}, u32[]{:S(2)}) collective-permute-start(f32[48,128]{1,0:T(8,128)S(1)} %contract.4.hr), channel_id=1, source_target_pairs={{0,16},{1,17},{2,18},{3,19},{4,20},{5,21},{6,22},{7,23},{8,24},{9,... | collective-permute-start | bytes 73736 | tf_op jit(solution)/shard_map/ppermute | solution.py:44
  41.0 0.0 collective-permute-done.6.src
  41.0 0.4 prep_far.1
  41.4 1.7 %contract.3 = (f32[96,128]{1,0:T(8,128)S(1)}, f32[48,128]{1,0:T(8,128)S(1)}) custom-call(f32[2048,128]{1,0:T(8,128)S(1)} %get-tuple-element.25.refs_0_, f32[1024,128]{1,0:T(8,128)S(1)} %get-tuple-element.28.refs_1_, bf16[3072,256]{1,0:T(8,128)(2,1)S(1)} %get-tuple-element.29.refs_2_.refs_1_.refs_3_, ...), custom_call_target="tpu_custom_call" | custom-call | tf_op jit(solution)/shard_map/contract/pallas_call | solution.py:318
  43.0 0.0 collective-permute-done.11.refs_0_
  43.0 0.6 %contract.5 = f32[96,128]{1,0:T(8,128)S(1)} custom-call(f32[1024,128]{1,0:T(8,128)S(1)} %collective-permute-done.11.refs_0_, bf16[3072,256]{1,0:T(8,128)(2,1)S(1)} %get-tuple-element.29.refs_2_.refs_1_.refs_3_, bf16[3072,256]{1,0:T(8,128)(2,1)S(1)} %get-tuple-element.30.refs_3_.refs_2_.refs_4_, ...), custom_call_target="tpu_custom_call" | custom-call | tf_op jit(solution)/shard_map/contract/pallas_call | solution.py:318
  43.7 0.0 collective-permute-start.12
  43.7 0.5 collective-permute-start.13
  44.2 7.6 %collective-permute-start.7 = (f32[96,128]{1,0:T(8,128)S(1)}, f32[96,128]{1,0:T(8,128)S(1)}, u32[]{:S(2)}, u32[]{:S(2)}) collective-permute-start(f32[96,128]{1,0:T(8,128)S(1)} %get-tuple-element.34), channel_id=1, source_target_pairs={{0,15},{1,0},{2,1},{3,2},{4,3},{5,4},{6,5},{7,6},{8,7},{9,8},{10,9... | collective-permute-start | bytes 147464 | tf_op jit(solution)/shard_map/ppermute | solution.py:44
  51.7 1.7 %collective-permute-start.8 = (f32[96,128]{1,0:T(8,128)S(1)}, f32[96,128]{1,0:T(8,128)S(1)}, u32[]{:S(2)}, u32[]{:S(2)}) collective-permute-start(f32[96,128]{1,0:T(8,128)S(1)} %get-tuple-element.34), channel_id=1, source_target_pairs={{0,31},{1,16},{2,17},{3,18},{4,19},{5,20},{6,21},{7,22},{8,23},{9,... | collective-permute-start | bytes 147464 | tf_op jit(solution)/shard_map/ppermute | solution.py:44
  53.4 0.0 collective-permute-done.14.rc
  53.5 0.0 collective-permute-start.9
  53.5 3.8 %collective-permute-done.9.oc = f32[48,128]{1,0:T(8,128)S(1)} collective-permute-done((f32[48,128]{1,0:T(8,128)S(1)}, f32[48,128]{1,0:T(8,128)S(1)}, u32[]{:S(2)}, u32[]{:S(2)}) %collective-permute-start.9) | collective-permute-done | bytes 24608 | tf_op jit(solution)/shard_map/ppermute | solution.py:44
  57.3 0.0 collective-permute-done.12.ra
  57.3 0.0 collective-permute-done.13.rb
  57.3 0.0 collective-permute-done.7.oa
  57.3 1.6 %collective-permute-done.8.ob = f32[96,128]{1,0:T(8,128)S(1)} collective-permute-done((f32[96,128]{1,0:T(8,128)S(1)}, f32[96,128]{1,0:T(8,128)S(1)}, u32[]{:S(2)}, u32[]{:S(2)}) %collective-permute-start.8) | collective-permute-done | bytes 49184 | tf_op jit(solution)/shard_map/ppermute | solution.py:44
  58.9 0.8 %finish.1 = f32[64,320]{1,0:T(8,128)} custom-call(f32[48,128]{1,0:T(8,128)S(1)} %get-tuple-element.33.refs_5_.ho, f32[96,128]{1,0:T(8,128)S(1)} %collective-permute-done.7.oa, f32[96,128]{1,0:T(8,128)S(1)} %collective-permute-done.8.ob, f32[48,128]{1,0:T(8,128)S(1)} %collective-permute-done.9.oc, f32[48,128]{1,0:T(8,128)S(1)} %contract.4.hr, ...), custom_call_target="tpu_custom_call" | custom-call | tf_op jit(solution)/shard_map/finish/pallas_call | solution.py:346
Async XLA Ops:
  0.0 4.3 %copy-start = (f32[96,256]{1,0:T(8,128)S(1)}, f32[96,256]{1,0:T(8,128)}, u32[]{:S(2)}) copy-start(f32[96,256]{1,0:T(8,128)} %refs_3_.1) | copy-start | bytes 294916
  1.2 39.8 %collective-permute-start.6 = (f32[1536,128]{1,0:T(8,128)S(1)}, f32[1536,128]{1,0:T(8,128)S(1)}, u32[]{:S(2)}, u32[]{:S(2)}) collective-permute-start(f32[1536,128]{1,0:T(8,128)S(1)} %head.1), channel_id=1, source_target_pairs={{0,16},{16,0},{1,17},{17,1},{2,18},{18,2},{3,19},{19,3},{4,20},{20... | collective-permute-start | bytes 2359304 | tf_op jit(solution)/shard_map/ppermute | solution.py:364
  4.3 7.4 %collective-permute-start.1 = (f32[96,256]{1,0:T(8,128)S(1)}, f32[96,256]{1,0:T(8,128)S(1)}, u32[]{:S(2)}, u32[]{:S(2)}) collective-permute-start(f32[96,256]{1,0:T(8,128)S(1)} %copy-done), channel_id=1, source_target_pairs={{0,2},{1,3},{2,4},{3,5},{4,6},{5,7},{6,8},{7,9},{8,10},{9,11},{10,... | collective-permute-start | bytes 294920 | tf_op jit(solution)/shard_map/ppermute | solution.py:52
  5.8 6.6 %collective-permute-start.4 = (f32[96,256]{1,0:T(8,128)S(1)}, f32[96,256]{1,0:T(8,128)S(1)}, u32[]{:S(2)}, u32[]{:S(2)}) collective-permute-start(f32[96,256]{1,0:T(8,128)S(1)} %copy-done), channel_id=1, source_target_pairs={{0,14},{1,15},{2,0},{3,1},{4,2},{5,3},{6,4},{7,5},{8,6},{9,7},{10,... | collective-permute-start | bytes 294920 | tf_op jit(solution)/shard_map/ppermute | solution.py:52
  9.0 8.0 %collective-permute-start = (f32[96,256]{1,0:T(8,128)S(1)}, f32[96,256]{1,0:T(8,128)S(1)}, u32[]{:S(2)}, u32[]{:S(2)}) collective-permute-start(f32[96,256]{1,0:T(8,128)S(1)} %copy-done), channel_id=1, source_target_pairs={{0,13},{1,4},{2,15},{3,6},{4,1},{5,8},{6,3},{7,10},{8,5},{9,12},{1... | collective-permute-start | bytes 294920 | tf_op jit(solution)/shard_map/ppermute | solution.py:52
  9.4 7.6 %collective-permute-start.3 = (f32[96,256]{1,0:T(8,128)S(1)}, f32[96,256]{1,0:T(8,128)S(1)}, u32[]{:S(2)}, u32[]{:S(2)}) collective-permute-start(f32[96,256]{1,0:T(8,128)S(1)} %copy-done), channel_id=1, source_target_pairs={{0,1},{1,0},{2,3},{3,2},{4,5},{5,4},{6,7},{7,6},{8,9},{9,8},{10,11... | collective-permute-start | bytes 294920 | tf_op jit(solution)/shard_map/ppermute | solution.py:52
  11.7 5.3 %collective-permute-start.2 = (f32[96,256]{1,0:T(8,128)S(1)}, f32[96,256]{1,0:T(8,128)S(1)}, u32[]{:S(2)}, u32[]{:S(2)}) collective-permute-start(f32[96,256]{1,0:T(8,128)S(1)} %collective-permute-done.1.refs_1_), channel_id=1, source_target_pairs={{0,1},{1,0},{2,3},{3,2},{4,5},{5,4},{6,7},{7,6},{8,9},{9,8},{10,11... | collective-permute-start | bytes 294920 | tf_op jit(solution)/shard_map/ppermute | solution.py:52
  12.4 4.7 %collective-permute-start.5 = (f32[96,256]{1,0:T(8,128)S(1)}, f32[96,256]{1,0:T(8,128)S(1)}, u32[]{:S(2)}, u32[]{:S(2)}) collective-permute-start(f32[96,256]{1,0:T(8,128)S(1)} %collective-permute-done.4.refs_5_), channel_id=1, source_target_pairs={{0,1},{1,0},{2,3},{3,2},{4,5},{5,4},{6,7},{7,6},{8,9},{9,8},{10,11... | collective-permute-start | bytes 294920 | tf_op jit(solution)/shard_map/ppermute | solution.py:52
  15.0 2.0 %copy-start.1 = (s32[1,1,3]{2,1,0:T(1,128)S(1)}, s32[1,1,3]{2,1,0:T(1,128)}, u32[]{:S(2)}) copy-start(s32[1,1,3]{2,1,0:T(1,128)} %refs_7_.1) | copy-start | bytes 40
  18.8 24.3 %collective-permute-start.11 = (f32[1024,128]{1,0:T(8,128)S(1)}, f32[1024,128]{1,0:T(8,128)S(1)}, u32[]{:S(2)}, u32[]{:S(2)}) collective-permute-start(f32[1024,128]{1,0:T(8,128)S(1)} %get-tuple-element.36), channel_id=1, source_target_pairs={{0,16},{16,0},{1,17},{17,1},{2,18},{18,2},{3,19},{19,3},{4,20},{20... | collective-permute-start | bytes 1572872 | tf_op jit(solution)/shard_map/ppermute | solution.py:372
  22.1 16.7 %collective-permute-start.10 = (f32[512,128]{1,0:T(8,128)S(1)}, f32[512,128]{1,0:T(8,128)S(1)}, u32[]{:S(2)}, u32[]{:S(2)}) collective-permute-start(f32[512,128]{1,0:T(8,128)S(1)} %get-tuple-element.35), channel_id=1, source_target_pairs={{0,16},{16,0},{1,17},{17,1},{2,18},{18,2},{3,19},{19,3},{4,20},{20... | collective-permute-start | bytes 786440 | tf_op jit(solution)/shard_map/ppermute | solution.py:375
  39.4 14.1 %collective-permute-start.14 = (f32[48,128]{1,0:T(8,128)S(1)}, f32[48,128]{1,0:T(8,128)S(1)}, u32[]{:S(2)}, u32[]{:S(2)}) collective-permute-start(f32[48,128]{1,0:T(8,128)S(1)} %contract.4.hr), channel_id=1, source_target_pairs={{0,16},{1,17},{2,18},{3,19},{4,20},{5,21},{6,22},{7,23},{8,24},{9,... | collective-permute-start | bytes 73736 | tf_op jit(solution)/shard_map/ppermute | solution.py:44
  43.7 13.6 %collective-permute-start.12 = (f32[96,128]{1,0:T(8,128)S(1)}, f32[96,128]{1,0:T(8,128)S(1)}, u32[]{:S(2)}, u32[]{:S(2)}) collective-permute-start(f32[96,128]{1,0:T(8,128)S(1)} %contract.5), channel_id=1, source_target_pairs={{0,1},{1,2},{2,3},{3,4},{4,5},{5,6},{6,7},{7,8},{8,9},{9,10},{10,1... | collective-permute-start | bytes 147464 | tf_op jit(solution)/shard_map/ppermute | solution.py:44
  43.7 13.6 %collective-permute-start.13 = (f32[96,128]{1,0:T(8,128)S(1)}, f32[96,128]{1,0:T(8,128)S(1)}, u32[]{:S(2)}, u32[]{:S(2)}) collective-permute-start(f32[96,128]{1,0:T(8,128)S(1)} %contract.5), channel_id=1, source_target_pairs={{0,17},{1,18},{2,19},{3,20},{4,21},{5,22},{6,23},{7,24},{8,25},{9,... | collective-permute-start | bytes 147464 | tf_op jit(solution)/shard_map/ppermute | solution.py:44
  44.2 13.1 %collective-permute-start.7 = (f32[96,128]{1,0:T(8,128)S(1)}, f32[96,128]{1,0:T(8,128)S(1)}, u32[]{:S(2)}, u32[]{:S(2)}) collective-permute-start(f32[96,128]{1,0:T(8,128)S(1)} %get-tuple-element.34), channel_id=1, source_target_pairs={{0,15},{1,0},{2,1},{3,2},{4,3},{5,4},{6,5},{7,6},{8,7},{9,8},{10,9... | collective-permute-start | bytes 147464 | tf_op jit(solution)/shard_map/ppermute | solution.py:44
  51.7 7.1 %collective-permute-start.8 = (f32[96,128]{1,0:T(8,128)S(1)}, f32[96,128]{1,0:T(8,128)S(1)}, u32[]{:S(2)}, u32[]{:S(2)}) collective-permute-start(f32[96,128]{1,0:T(8,128)S(1)} %get-tuple-element.34), channel_id=1, source_target_pairs={{0,31},{1,16},{2,17},{3,18},{4,19},{5,20},{6,21},{7,22},{8,23},{9,... | collective-permute-start | bytes 147464 | tf_op jit(solution)/shard_map/ppermute | solution.py:44
  53.5 3.8 %collective-permute-start.9 = (f32[48,128]{1,0:T(8,128)S(1)}, f32[48,128]{1,0:T(8,128)S(1)}, u32[]{:S(2)}, u32[]{:S(2)}) collective-permute-start(f32[48,128]{1,0:T(8,128)S(1)} %get-tuple-element.33.refs_5_.ho), channel_id=1, source_target_pairs={{0,16},{1,17},{2,18},{3,19},{4,20},{5,21},{6,22},{7,23},{8,24},{9,... | collective-permute-start | bytes 73736 | tf_op jit(solution)/shard_map/ppermute | solution.py:44
